TPU v7x, 256 devices: a whole 4x4x8 slice. The times are simulated.
256 devices in a mesh: node: 32 (over z_hi, x, core), ctrl: 8 (over y, z_lo).
Axes of the slice: x: 4, y: 4, z: 8 (z_hi: 4, z_lo: 2; z = z_hi * 2 + z_lo), core: 2. Of those that a mesh axis runs over, the one named last changes fastest.
Arguments:
- sensitivity: bfloat16 [96, 131072], P(None, 'node'), may hold values from -1 to 1
- node_xyz: float32 [3, 131072], P(None, 'node'), may hold values from 0 to 1
- ctrl_xyz: float32 [3, 16384], P(None, 'ctrl'), may hold values from 0 to 1
- inverse: bfloat16 [16384, 16384], P('ctrl', 'node'), may hold values from -0.046875 to 0.046875
Outputs:
- control_grad: float32 [96, 16384], P(None, ('node', 'ctrl'))
All inputs are finite; a program needn't handle non-finite values.
Results may differ from a plain program's by a relative error of at most 0.004.
Values may be sent and summed in bfloat16 or wider, within the bound.
No kernel may reach another device: no remote copies, remote signals or barrier semaphores. Data moves between devices by JAX's collectives and lax.ppermute only.
A program may use at most 64 MiB of HBM per device.

v0:
```python
import functools

import jax
import jax.numpy as jnp
from jax import lax
from jax.experimental import pallas as pl
from jax.experimental.pallas import tpu as pltpu
from jax.sharding import Mesh, PartitionSpec as P


support_radius = 0.12
stretch = 4.0 / support_radius
depth = 128
span = 256
whole = pl.BlockSpec(memory_space=pltpu.VMEM)
params = pltpu.CompilerParams(vmem_limit_bytes=16 * 1024 * 1024)


def pieces_of(values):
    high = values.astype(jnp.bfloat16).astype(jnp.float32)
    rest = values - high
    middle = rest.astype(jnp.bfloat16).astype(jnp.float32)
    low = (rest - middle).astype(jnp.bfloat16).astype(jnp.float32)
    return high, middle, low


def write_features(xyz_ref, rows, is_node):
    count = xyz_ref.shape[1]
    place = (xyz_ref[...] - 0.5) * stretch
    norm = (
        place[0:1] * place[0:1] + place[1:2] * place[1:2] + place[2:3] * place[2:3]
    )
    parts = pieces_of(place)
    norm_parts = pieces_of(norm)
    ones = jnp.ones((3, count), jnp.float32)
    rows[...] = jnp.zeros_like(rows)
    for i in range(3):
        for j in range(3):
            k = 3 * (3 * i + j)
            rows[k : k + 3, :] = parts[i] if is_node else -2.0 * parts[j]
    norm_at, ones_at = (27, 30) if is_node else (30, 27)
    rows[ones_at : ones_at + 3, :] = ones
    for i in range(3):
        rows[norm_at + i : norm_at + i + 1, :] = norm_parts[i]


def wendland(squared):
    squared = jnp.maximum(squared, 1e-30)
    r4 = squared * lax.rsqrt(squared)
    remain = jnp.maximum(4.0 - r4, 0.0)
    remain2 = remain * remain
    return (remain2 * remain2 * (r4 + 1.0)).astype(jnp.bfloat16)


def pulled_block(node_ref, ctrl_ref, sens_ref, block):
    columns = pl.ds(pl.multiple_of(block * span, span), span)
    squared = jnp.dot(
        node_ref[...], ctrl_ref[:, columns], preferred_element_type=jnp.float32
    )
    total = jnp.dot(
        sens_ref[...], wendland(squared), preferred_element_type=jnp.float32
    )
    return total * (1.0 / 256.0)


def first_kernel(
    by, sens_in, node_in, ctrl_in, out_ref, node_ref, ctrl_ref, sens_ref, *scratch
):
    node_xyz, ctrl_xyz, node_rows, ctrl_rows, done = scratch
    copies = [
        pltpu.make_async_copy(source, target, done.at[i])
        for i, (source, target) in enumerate(
            ((node_in, node_xyz), (ctrl_in, ctrl_xyz), (sens_in, sens_ref))
        )
    ]
    for copy in copies:
        copy.start()
    copies[0].wait()
    write_features(node_xyz, node_rows, True)
    node_ref[...] = node_rows[...].T.astype(jnp.bfloat16)
    copies[1].wait()
    write_features(ctrl_xyz, ctrl_rows, False)
    ctrl_ref[...] = ctrl_rows[...].astype(jnp.bfloat16)
    copies[2].wait()
    block = (1 - lax.axis_index("core")) * 4 + lax.bitwise_xor(lax.axis_index("x"), by)
    out_ref[...] = pulled_block(node_ref, ctrl_ref, sens_ref, block)


def pull_cost(nodes, blocks):
    return pl.CostEstimate(
        flops=blocks * span * nodes * 400,
        bytes_accessed=nodes * 448,
        transcendentals=blocks * span * nodes,
    )


def first_pull(by, sens, node_xyz, ctrl_xyz):
    rows, nodes = sens.shape
    ctrls = ctrl_xyz.shape[1]
    return pl.pallas_call(
        functools.partial(first_kernel, by),
        out_shape=[
            jax.ShapeDtypeStruct((rows, span), jnp.float32),
            jax.ShapeDtypeStruct((nodes, depth), jnp.bfloat16),
            jax.ShapeDtypeStruct((depth, ctrls), jnp.bfloat16),
            jax.ShapeDtypeStruct(sens.shape, sens.dtype),
        ],
        in_specs=[pl.BlockSpec(memory_space=pltpu.HBM)] * 3,
        out_specs=[whole] * 4,
        scratch_shapes=[
            pltpu.VMEM(node_xyz.shape, jnp.float32),
            pltpu.VMEM(ctrl_xyz.shape, jnp.float32),
            pltpu.VMEM((depth, nodes), jnp.float32),
            pltpu.VMEM((depth, ctrls), jnp.float32),
            pltpu.SemaphoreType.DMA((3,)),
        ],
        cost_estimate=pull_cost(nodes, 2),
        compiler_params=params,
        name="first_pull",
    )(*(pltpu.with_memory_space_constraint(a, pltpu.HBM) for a in (sens, node_xyz, ctrl_xyz)))


def pull_kernel(other, steps, add_at, node_ref, ctrl_ref, sens_ref, *rest):
    out_ref = rest[-1]
    core = lax.axis_index("core")
    x = lax.axis_index("x")
    half = (1 - core) if other else core
    if len(steps) == 1:
        block = half * 4 + lax.bitwise_xor(x, steps[0])
        total = pulled_block(node_ref, ctrl_ref, sens_ref, block)
        if len(rest) == 2:
            total = total + rest[0][:, add_at * span : (add_at + 1) * span]
        out_ref[...] = total
        return

    def body(j, carry):
        block = half * 4 + lax.bitwise_xor(x, steps[0] + j * (steps[1] - steps[0]))
        columns = pl.ds(pl.multiple_of(j * span, span), span)
        out_ref[:, columns] = pulled_block(node_ref, ctrl_ref, sens_ref, block)
        return carry

    lax.fori_loop(0, len(steps), body, 0)


def pull(prepared, other, steps, add=None, add_at=0):
    rows, nodes = prepared[2].shape
    args = list(prepared) + ([] if add is None else [add])
    return pl.pallas_call(
        functools.partial(pull_kernel, other, steps, add_at),
        out_shape=jax.ShapeDtypeStruct((rows, len(steps) * span), jnp.float32),
        in_specs=[whole] * len(args),
        out_specs=whole,
        cost_estimate=pull_cost(nodes, len(steps)),
        compiler_params=params,
        name="pull",
    )(*args)


def product_kernel(order, *refs):
    blocks, inverse_ref, out_ref = refs[:-2], refs[-2], refs[-1]
    core = lax.axis_index("core")
    x = lax.axis_index("x")
    total = None
    for half, joined in ((core, blocks[:-1]), (1 - core, blocks[-1:])):
        for i, by in enumerate(order):
            at = pl.multiple_of((half * 4 + lax.bitwise_xor(x, by)) * span, span)
            if len(joined) == 1:
                block = joined[0][:, i * span : (i + 1) * span]
            else:
                block = joined[i][...]
            term = jnp.dot(
                block,
                inverse_ref[pl.ds(at, span), :],
                preferred_element_type=jnp.float32,
            )
            total = term if total is None else total + term
    shares, rows, lanes = out_ref.shape
    width = lanes // 2
    for j in range(shares):
        share = total[:, j * width : (j + 1) * width]
        out_ref[j] = jnp.concatenate([share[:rows], share[rows:]], axis=1).astype(
            out_ref.dtype
        )


def product(order, blocks, inverse, shares):
    rows, width = blocks[0].shape[0], inverse.shape[1] // shares
    return pl.pallas_call(
        functools.partial(product_kernel, order),
        out_shape=jax.ShapeDtypeStruct((shares, rows // 2, 2 * width), jnp.bfloat16),
        in_specs=[whole] * (len(blocks) + 1),
        out_specs=whole,
        compiler_params=params,
        name="product",
    )(*blocks, inverse)


def finish_kernel(shares_ref, out_ref):
    total = shares_ref[0].astype(jnp.float32)
    for j in range(1, shares_ref.shape[0]):
        total = total + shares_ref[j].astype(jnp.float32)
    rows, lanes = total.shape
    turned = total.T
    out_ref[:, 0:rows] = turned[: lanes // 2]
    out_ref[:, rows:] = turned[lanes // 2 :]


def finish(shares):
    _, rows, lanes = shares.shape
    return pl.pallas_call(
        finish_kernel,
        out_shape=jax.ShapeDtypeStruct((lanes // 2, 2 * rows), jnp.float32),
        in_specs=[whole],
        out_specs=whole,
        compiler_params=params,
        name="finish",
    )(shares).T


def swapped(value, axis, by):
    size = lax.axis_size(axis)
    return lax.ppermute(value, axis, [(i, i ^ by) for i in range(size)])


def per_device(sensitivity, node_xyz, ctrl_xyz, inverse):
    def pulled(*args):
        return pull(prepared, *args)

    first, *prepared = first_pull(2, sensitivity, node_xyz, ctrl_xyz)
    first = swapped(first, "core", 1)
    second = swapped(pulled(True, (1, 3)), "core", 1)
    parts = [
        swapped(pulled(False, (2,), first), "x", 2),
        swapped(pulled(False, (1,), second, 0), "x", 1),
        swapped(pulled(False, (3,), second, 1), "x", 3),
        swapped(pulled(True, (0,)), "core", 1),
    ]
    summed = pulled(False, (0,))
    for part in parts:
        summed = summed + part

    low = summed.astype(jnp.bfloat16)
    for by in (2, 1, 3):
        summed = summed + swapped(low, "zh", by).astype(jnp.float32)
    mine = summed.astype(jnp.bfloat16)

    order = (2, 1, 3)
    along_x = [mine] + [swapped(mine, "x", by) for by in order]
    across = swapped(jnp.concatenate(along_x, axis=1), "core", 1)
    shares = product((0,) + order, along_x + [across], inverse, 8)
    arrived_shares = lax.all_to_all(
        shares, ("y", "zl"), split_axis=0, concat_axis=0, tiled=True
    )
    return finish(arrived_shares)


def solution(mesh):
    fine = Mesh(
        mesh.devices.reshape(4, 4, 2, 4, 2), ("zh", "x", "core", "y", "zl")
    )
    node, ctrl = ("zh", "x", "core"), ("y", "zl")
    in_specs = (P(None, node), P(None, node), P(None, ctrl), P(ctrl, node))
    out_specs = P(None, node + ctrl)

    return jax.shard_map(
        per_device, mesh=fine, in_specs=in_specs, out_specs=out_specs, check_vma=False
    )
```

profile of v0, /device:TPU:1, one launch (start us, length us, event | category | flops | bytes accessed | tf_op | source)
XLA Modules:
  0.0 60.8 jit_solution(583299044079653628)
XLA Ops:
  0.0 3.3 %first_pull.1 = (f32[96,256]{1,0:T(8,128)S(1)}, bf16[4096,128]{1,0:T(8,128)(2,1)S(1)}, bf16[128,2048]{1,0:T(8,128)(2,1)S(1)}, bf16[96,4096]{1,0:T(8,128)(2,1)S(1)}) custom-call(bf16[96,4096]{1,0:T(8,128)(2,1)} %sens_in.1, f32[3,4096]{1,0:T(4,128)} %node_in.1, f32[3,2048]{1,0:T(4,128)} %ctrl_in.1), custom_call_target="tpu_custom_call" | custom-call | flops 838860800 | bytes 1835008 | tf_op jit(solution)/shard_map/first_pull/pallas_call | solution.py:100
  3.3 3.6 %pull.8 = f32[96,512]{1,0:T(8,128)S(1)} custom-call(bf16[4096,128]{1,0:T(8,128)(2,1)S(1)} %get-tuple-element.9.node_ref, bf16[128,2048]{1,0:T(8,128)(2,1)S(1)} %get-tuple-element.10.ctrl_ref, bf16[96,4096]{1,0:T(8,128)(2,1)S(1)} %get-tuple-element.11.sens_ref), custom_call_target="tpu_custom_call" | custom-call | flops 838860800 | bytes 1835008 | tf_op jit(solution)/shard_map/pull/pallas_call | solution.py:148
  7.0 3.3 %collective-permute-start.2 = (f32[96,512]{1,0:T(8,128)S(1)}, f32[96,512]{1,0:T(8,128)S(1)}, u32[]{:S(2)}, u32[]{:S(2)}) collective-permute-start(f32[96,512]{1,0:T(8,128)S(1)} %pull.8), channel_id=1, source_target_pairs={{0,8},{8,0},{1,9},{9,1},{2,10},{10,2},{3,11},{11,3},{4,12},{12,4},... | collective-permute-start | bytes 589832 | tf_op jit(solution)/shard_map/ppermute | solution.py:222
  10.3 1.8 %pull.11 = f32[96,256]{1,0:T(8,128)S(1)} custom-call(bf16[4096,128]{1,0:T(8,128)(2,1)S(1)} %get-tuple-element.9.node_ref, bf16[128,2048]{1,0:T(8,128)(2,1)S(1)} %get-tuple-element.10.ctrl_ref, bf16[96,4096]{1,0:T(8,128)(2,1)S(1)} %get-tuple-element.11.sens_ref), custom_call_target="tpu_custom_call" | custom-call | flops 419430400 | bytes 1835008 | tf_op jit(solution)/shard_map/pull/pallas_call | solution.py:148
  12.7 1.8 %pull.7 = f32[96,256]{1,0:T(8,128)S(1)} custom-call(bf16[4096,128]{1,0:T(8,128)(2,1)S(1)} %get-tuple-element.9.node_ref, bf16[128,2048]{1,0:T(8,128)(2,1)S(1)} %get-tuple-element.10.ctrl_ref, bf16[96,4096]{1,0:T(8,128)(2,1)S(1)} %get-tuple-element.11.sens_ref, f32[96,256]{1,0:T(8,128)S(1)} %collective-permute-done.rest_0_), custom_call_target="tpu_custom_call" | custom-call | flops 419430400 | bytes 1835008 | tf_op jit(solution)/shard_map/pull/pallas_call | solution.py:148
  14.5 1.1 %collective-permute-start.1 = (f32[96,256]{1,0:T(8,128)S(1)}, f32[96,256]{1,0:T(8,128)S(1)}, u32[]{:S(2)}, u32[]{:S(2)}) collective-permute-start(f32[96,256]{1,0:T(8,128)S(1)} %pull.7), channel_id=1, source_target_pairs={{0,32},{16,48},{32,0},{48,16},{1,33},{17,49},{33,1},{49,17},{2,34}... | collective-permute-start | bytes 294920 | tf_op jit(solution)/shard_map/ppermute | solution.py:222
  15.6 1.8 %pull.9 = f32[96,256]{1,0:T(8,128)S(1)} custom-call(bf16[4096,128]{1,0:T(8,128)(2,1)S(1)} %get-tuple-element.9.node_ref, bf16[128,2048]{1,0:T(8,128)(2,1)S(1)} %get-tuple-element.10.ctrl_ref, bf16[96,4096]{1,0:T(8,128)(2,1)S(1)} %get-tuple-element.11.sens_ref, f32[96,512]{1,0:T(8,128)S(1)} %collective-permute-done.2.rest_0_), custom_call_target="tpu_custom_call" | custom-call | flops 419430400 | bytes 1835008 | tf_op jit(solution)/shard_map/pull/pallas_call | solution.py:148
  17.4 0.6 collective-permute-start.3
  18.0 1.8 %pull.10 = f32[96,256]{1,0:T(8,128)S(1)} custom-call(bf16[4096,128]{1,0:T(8,128)(2,1)S(1)} %get-tuple-element.9.node_ref, bf16[128,2048]{1,0:T(8,128)(2,1)S(1)} %get-tuple-element.10.ctrl_ref, bf16[96,4096]{1,0:T(8,128)(2,1)S(1)} %get-tuple-element.11.sens_ref, f32[96,512]{1,0:T(8,128)S(1)} %collective-permute-done.2.rest_0_), custom_call_target="tpu_custom_call" | custom-call | flops 419430400 | bytes 1835008 | tf_op jit(solution)/shard_map/pull/pallas_call | solution.py:148
  19.8 2.0 %collective-permute-start.4 = (f32[96,256]{1,0:T(8,128)S(1)}, f32[96,256]{1,0:T(8,128)S(1)}, u32[]{:S(2)}, u32[]{:S(2)}) collective-permute-start(f32[96,256]{1,0:T(8,128)S(1)} %pull.10), channel_id=1, source_target_pairs={{0,48},{16,32},{32,16},{48,0},{1,49},{17,33},{33,17},{49,1},{2,50}... | collective-permute-start | bytes 294920 | tf_op jit(solution)/shard_map/ppermute | solution.py:222
  21.8 1.8 %pull.6 = f32[96,256]{1,0:T(8,128)S(1)} custom-call(bf16[4096,128]{1,0:T(8,128)(2,1)S(1)} %get-tuple-element.9.node_ref, bf16[128,2048]{1,0:T(8,128)(2,1)S(1)} %get-tuple-element.10.ctrl_ref, bf16[96,4096]{1,0:T(8,128)(2,1)S(1)} %get-tuple-element.11.sens_ref), custom_call_target="tpu_custom_call" | custom-call | flops 419430400 | bytes 1835008 | tf_op jit(solution)/shard_map/pull/pallas_call | solution.py:148
  23.7 0.9 %collective-permute-done.4 = f32[96,256]{1,0:T(8,128)S(1)} collective-permute-done((f32[96,256]{1,0:T(8,128)S(1)}, f32[96,256]{1,0:T(8,128)S(1)}, u32[]{:S(2)}, u32[]{:S(2)}) %collective-permute-start.4) | collective-permute-done | bytes 98336 | tf_op jit(solution)/shard_map/ppermute | solution.py:222
  24.6 7.0 %collective-permute-start.6 = (bf16[96,256]{1,0:T(8,128)(2,1)S(1)}, bf16[96,256]{1,0:T(8,128)(2,1)S(1)}, u32[]{:S(2)}, u32[]{:S(2)}) collective-permute-start(bf16[96,256]{1,0:T(8,128)(2,1)S(1)} %get-tuple-element.13), channel_id=1, source_target_pairs={{0,128},{64,192},{128,0},{192,64},{1,129},{65,193},{129,1},{193,65... | collective-permute-start | bytes 147464 | tf_op jit(solution)/shard_map/ppermute | solution.py:222
  31.6 1.2 %collective-permute-start.7 = (bf16[96,256]{1,0:T(8,128)(2,1)S(1)}, bf16[96,256]{1,0:T(8,128)(2,1)S(1)}, u32[]{:S(2)}, u32[]{:S(2)}) collective-permute-start(bf16[96,256]{1,0:T(8,128)(2,1)S(1)} %get-tuple-element.13), channel_id=1, source_target_pairs={{0,64},{64,0},{128,192},{192,128},{1,65},{65,1},{129,193},{193,129... | collective-permute-start | bytes 147464 | tf_op jit(solution)/shard_map/ppermute | solution.py:222
  33.1 3.9 %collective-permute-done.7 = bf16[96,256]{1,0:T(8,128)(2,1)S(1)} collective-permute-done((bf16[96,256]{1,0:T(8,128)(2,1)S(1)}, bf16[96,256]{1,0:T(8,128)(2,1)S(1)}, u32[]{:S(2)}, u32[]{:S(2)}) %collective-permute-start.7) | collective-permute-done | bytes 49184 | tf_op jit(solution)/shard_map/ppermute | solution.py:222
  37.1 1.3 %collective-permute-done.8 = bf16[96,256]{1,0:T(8,128)(2,1)S(1)} collective-permute-done((bf16[96,256]{1,0:T(8,128)(2,1)S(1)}, bf16[96,256]{1,0:T(8,128)(2,1)S(1)}, u32[]{:S(2)}, u32[]{:S(2)}) %collective-permute-start.8) | collective-permute-done | bytes 49184 | tf_op jit(solution)/shard_map/ppermute | solution.py:222
  38.5 0.9 %collective-permute-start.11 = (bf16[96,256]{1,0:T(8,128)(2,1)S(1)}, bf16[96,256]{1,0:T(8,128)(2,1)S(1)}, u32[]{:S(2)}, u32[]{:S(2)}) collective-permute-start(bf16[96,256]{1,0:T(8,128)(2,1)S(1)} %add_convert_fusion.refs_0_), channel_id=1, source_target_pairs={{0,48},{16,32},{32,16},{48,0},{1,49},{17,33},{33,17},{49,1},{2,50}... | collective-permute-start | bytes 147464 | tf_op jit(solution)/shard_map/ppermute | solution.py:222
  39.4 2.4 %collective-permute-start.9 = (bf16[96,256]{1,0:T(8,128)(2,1)S(1)}, bf16[96,256]{1,0:T(8,128)(2,1)S(1)}, u32[]{:S(2)}, u32[]{:S(2)}) collective-permute-start(bf16[96,256]{1,0:T(8,128)(2,1)S(1)} %add_convert_fusion.refs_0_), channel_id=1, source_target_pairs={{0,32},{16,48},{32,0},{48,16},{1,33},{17,49},{33,1},{49,17},{2,34}... | collective-permute-start | bytes 147464 | tf_op jit(solution)/shard_map/ppermute | solution.py:222
  41.8 1.0 %collective-permute-done.11.refs_3_ = bf16[96,256]{1,0:T(8,128)(2,1)S(1)} collective-permute-done((bf16[96,256]{1,0:T(8,128)(2,1)S(1)}, bf16[96,256]{1,0:T(8,128)(2,1)S(1)}, u32[]{:S(2)}, u32[]{:S(2)}) %collective-permute-start.11) | collective-permute-done | bytes 49184 | tf_op jit(solution)/shard_map/ppermute | solution.py:222
  42.8 1.1 %collective-permute-done.9.refs_1_ = bf16[96,256]{1,0:T(8,128)(2,1)S(1)} collective-permute-done((bf16[96,256]{1,0:T(8,128)(2,1)S(1)}, bf16[96,256]{1,0:T(8,128)(2,1)S(1)}, u32[]{:S(2)}, u32[]{:S(2)}) %collective-permute-start.9) | collective-permute-done | bytes 49184 | tf_op jit(solution)/shard_map/ppermute | solution.py:222
  43.9 4.8 %collective-permute-start.12 = (bf16[96,1024]{1,0:T(8,128)(2,1)S(1)}, bf16[96,1024]{1,0:T(8,128)(2,1)S(1)}, u32[]{:S(2)}, u32[]{:S(2)}) collective-permute-start(bf16[96,1024]{1,0:T(8,128)(2,1)S(1)} %pad_maximum_fusion), channel_id=1, source_target_pairs={{0,8},{8,0},{1,9},{9,1},{2,10},{10,2},{3,11},{11,3},{4,12},{12,4},... | collective-permute-start | bytes 589832 | tf_op jit(solution)/shard_map/ppermute | solution.py:222
  48.6 1.1 %collective-permute-done.12.refs_4_ = bf16[96,1024]{1,0:T(8,128)(2,1)S(1)} collective-permute-done((bf16[96,1024]{1,0:T(8,128)(2,1)S(1)}, bf16[96,1024]{1,0:T(8,128)(2,1)S(1)}, u32[]{:S(2)}, u32[]{:S(2)}) %collective-permute-start.12) | collective-permute-done | bytes 196640 | tf_op jit(solution)/shard_map/ppermute | solution.py:222
  50.3 9.7 %all_to_all.5.shares_ref = bf16[8,48,128]{2,1,0:T(8,128)(2,1)S(1)} all-to-all(bf16[8,48,128]{2,1,0:T(8,128)(2,1)S(1)} %product.1), channel_id=1, replica_groups=mesh['zh'=4,'x'=4,'core'=2,'y'=4,'zl'=2] {'y','zl'}, dimensions={0} | all-to-all | bytes 196608 | tf_op jit(solution)/shard_map/all_to_all | solution.py:251
  60.0 0.8 %finish.1 = f32[64,96]{1,0:T(8,128)} custom-call(bf16[8,48,128]{2,1,0:T(8,128)(2,1)S(1)} %all_to_all.5.shares_ref), custom_call_target="tpu_custom_call" | custom-call | tf_op jit(solution)/shard_map/finish/pallas_call | solution.py:210
  (17 shorter events, 1.6 us)
Async XLA Ops:
  7.0 8.6 %collective-permute-start.2 = (f32[96,512]{1,0:T(8,128)S(1)}, f32[96,512]{1,0:T(8,128)S(1)}, u32[]{:S(2)}, u32[]{:S(2)}) collective-permute-start(f32[96,512]{1,0:T(8,128)S(1)} %pull.8), channel_id=1, source_target_pairs={{0,8},{8,0},{1,9},{9,1},{2,10},{10,2},{3,11},{11,3},{4,12},{12,4},... | collective-permute-start | bytes 589832 | tf_op jit(solution)/shard_map/ppermute | solution.py:222
  10.2 2.4 %collective-permute-start = (f32[96,256]{1,0:T(8,128)S(1)}, f32[96,256]{1,0:T(8,128)S(1)}, u32[]{:S(2)}, u32[]{:S(2)}) collective-permute-start(f32[96,256]{1,0:T(8,128)S(1)} %get-tuple-element.12), channel_id=1, source_target_pairs={{0,8},{8,0},{1,9},{9,1},{2,10},{10,2},{3,11},{11,3},{4,12},{12,4},... | collective-permute-start | bytes 294920 | tf_op jit(solution)/shard_map/ppermute | solution.py:222
  12.2 11.5 %collective-permute-start.5 = (f32[96,256]{1,0:T(8,128)S(1)}, f32[96,256]{1,0:T(8,128)S(1)}, u32[]{:S(2)}, u32[]{:S(2)}) collective-permute-start(f32[96,256]{1,0:T(8,128)S(1)} %pull.11), channel_id=1, source_target_pairs={{0,8},{8,0},{1,9},{9,1},{2,10},{10,2},{3,11},{11,3},{4,12},{12,4},... | collective-permute-start | bytes 294920 | tf_op jit(solution)/shard_map/ppermute | solution.py:222
  14.5 9.2 %collective-permute-start.1 = (f32[96,256]{1,0:T(8,128)S(1)}, f32[96,256]{1,0:T(8,128)S(1)}, u32[]{:S(2)}, u32[]{:S(2)}) collective-permute-start(f32[96,256]{1,0:T(8,128)S(1)} %pull.7), channel_id=1, source_target_pairs={{0,32},{16,48},{32,0},{48,16},{1,33},{17,49},{33,1},{49,17},{2,34}... | collective-permute-start | bytes 294920 | tf_op jit(solution)/shard_map/ppermute | solution.py:222
  17.4 6.3 %collective-permute-start.3 = (f32[96,256]{1,0:T(8,128)S(1)}, f32[96,256]{1,0:T(8,128)S(1)}, u32[]{:S(2)}, u32[]{:S(2)}) collective-permute-start(f32[96,256]{1,0:T(8,128)S(1)} %pull.9), channel_id=1, source_target_pairs={{0,16},{16,0},{32,48},{48,32},{1,17},{17,1},{33,49},{49,33},{2,18}... | collective-permute-start | bytes 294920 | tf_op jit(solution)/shard_map/ppermute | solution.py:222
  19.8 29.9 %copy-start = (bf16[2048,512]{1,0:T(8,128)(2,1)S(1)}, bf16[2048,512]{1,0:T(8,128)(2,1)}, u32[]{:S(2)}) copy-start(bf16[2048,512]{1,0:T(8,128)(2,1)} %refs_5_.1) | copy-start | bytes 6291460
  19.8 4.8 %collective-permute-start.4 = (f32[96,256]{1,0:T(8,128)S(1)}, f32[96,256]{1,0:T(8,128)S(1)}, u32[]{:S(2)}, u32[]{:S(2)}) collective-permute-start(f32[96,256]{1,0:T(8,128)S(1)} %pull.10), channel_id=1, source_target_pairs={{0,48},{16,32},{32,16},{48,0},{1,49},{17,33},{33,17},{49,1},{2,50}... | collective-permute-start | bytes 294920 | tf_op jit(solution)/shard_map/ppermute | solution.py:222
  24.6 8.5 %collective-permute-start.6 = (bf16[96,256]{1,0:T(8,128)(2,1)S(1)}, bf16[96,256]{1,0:T(8,128)(2,1)S(1)}, u32[]{:S(2)}, u32[]{:S(2)}) collective-permute-start(bf16[96,256]{1,0:T(8,128)(2,1)S(1)} %get-tuple-element.13), channel_id=1, source_target_pairs={{0,128},{64,192},{128,0},{192,64},{1,129},{65,193},{129,1},{193,65... | collective-permute-start | bytes 147464 | tf_op jit(solution)/shard_map/ppermute | solution.py:222
  31.6 5.4 %collective-permute-start.7 = (bf16[96,256]{1,0:T(8,128)(2,1)S(1)}, bf16[96,256]{1,0:T(8,128)(2,1)S(1)}, u32[]{:S(2)}, u32[]{:S(2)}) collective-permute-start(bf16[96,256]{1,0:T(8,128)(2,1)S(1)} %get-tuple-element.13), channel_id=1, source_target_pairs={{0,64},{64,0},{128,192},{192,128},{1,65},{65,1},{129,193},{193,129... | collective-permute-start | bytes 147464 | tf_op jit(solution)/shard_map/ppermute | solution.py:222
  32.8 5.5 %collective-permute-start.8 = (bf16[96,256]{1,0:T(8,128)(2,1)S(1)}, bf16[96,256]{1,0:T(8,128)(2,1)S(1)}, u32[]{:S(2)}, u32[]{:S(2)}) collective-permute-start(bf16[96,256]{1,0:T(8,128)(2,1)S(1)} %get-tuple-element.13), channel_id=1, source_target_pairs={{0,192},{64,128},{128,64},{192,0},{1,193},{65,129},{129,65},{193,1... | collective-permute-start | bytes 147464 | tf_op jit(solution)/shard_map/ppermute | solution.py:222
  38.4 3.3 %collective-permute-start.10 = (bf16[96,256]{1,0:T(8,128)(2,1)S(1)}, bf16[96,256]{1,0:T(8,128)(2,1)S(1)}, u32[]{:S(2)}, u32[]{:S(2)}) collective-permute-start(bf16[96,256]{1,0:T(8,128)(2,1)S(1)} %add_convert_fusion.refs_0_), channel_id=1, source_target_pairs={{0,16},{16,0},{32,48},{48,32},{1,17},{17,1},{33,49},{49,33},{2,18}... | collective-permute-start | bytes 147464 | tf_op jit(solution)/shard_map/ppermute | solution.py:222
  38.5 4.2 %collective-permute-start.11 = (bf16[96,256]{1,0:T(8,128)(2,1)S(1)}, bf16[96,256]{1,0:T(8,128)(2,1)S(1)}, u32[]{:S(2)}, u32[]{:S(2)}) collective-permute-start(bf16[96,256]{1,0:T(8,128)(2,1)S(1)} %add_convert_fusion.refs_0_), channel_id=1, source_target_pairs={{0,48},{16,32},{32,16},{48,0},{1,49},{17,33},{33,17},{49,1},{2,50}... | collective-permute-start | bytes 147464 | tf_op jit(solution)/shard_map/ppermute | solution.py:222
  39.4 4.4 %collective-permute-start.9 = (bf16[96,256]{1,0:T(8,128)(2,1)S(1)}, bf16[96,256]{1,0:T(8,128)(2,1)S(1)}, u32[]{:S(2)}, u32[]{:S(2)}) collective-permute-start(bf16[96,256]{1,0:T(8,128)(2,1)S(1)} %add_convert_fusion.refs_0_), channel_id=1, source_target_pairs={{0,32},{16,48},{32,0},{48,16},{1,33},{17,49},{33,1},{49,17},{2,34}... | collective-permute-start | bytes 147464 | tf_op jit(solution)/shard_map/ppermute | solution.py:222
  43.9 5.9 %collective-permute-start.12 = (bf16[96,1024]{1,0:T(8,128)(2,1)S(1)}, bf16[96,1024]{1,0:T(8,128)(2,1)S(1)}, u32[]{:S(2)}, u32[]{:S(2)}) collective-permute-start(bf16[96,1024]{1,0:T(8,128)(2,1)S(1)} %pad_maximum_fusion), channel_id=1, source_target_pairs={{0,8},{8,0},{1,9},{9,1},{2,10},{10,2},{3,11},{11,3},{4,12},{12,4},... | collective-permute-start | bytes 589832 | tf_op jit(solution)/shard_map/ppermute | solution.py:222
where the time goes:
time: 61 us; the launch traced here: 60.8 us
  starting transfers between devices  23.9 us (39%)
  Pallas kernels  17.3 us (28%)
  blocking collectives  9.74 us (16%)
  waiting for transfers between devices  9.62 us (16%)
    ppermute x13, starting transfers between devices, swapped(): return lax.ppermute(value, axis, [(i, i ^ by) for i in range(size)])  23.9 us
    pallas_call x6, Pallas kernels, pull(): pl.pallas_call(functools.partial(pull_kernel, other, steps, add_at), out_...  12.7 us
    all_to_all x1, blocking collectives, per_device(): lax.all_to_all(shares, ('y', 'zl'), split_axis=0, concat_axis=0, tiled=True)  9.74 us
    ppermute x13, waiting for transfers between devices, swapped(): return lax.ppermute(value, axis, [(i, i ^ by) for i in range(size)])  9.62 us
    pallas_call x1, Pallas kernels, first_pull(): pl.pallas_call(functools.partial(first_kernel, by), out_shape=[jax.ShapeD...  3.3 us
  transfers between devices with their start and end apart: 13, of which 7 were waited for; matrix products, arithmetic and copies ran while one was open for 0% of the time, Pallas kernels for 15%

commit v1 on v0

--- a/solution.py
+++ b/solution.py
@@ -11,6 +11,7 @@
 support_radius = 0.12
 stretch = 4.0 / support_radius
 depth = 128
+used = 40
 span = 256
 whole = pl.BlockSpec(memory_space=pltpu.VMEM)
 params = pltpu.CompilerParams(vmem_limit_bytes=16 * 1024 * 1024)
@@ -64,7 +65,7 @@
 
 
 def first_kernel(
-    by, sens_in, node_in, ctrl_in, out_ref, node_ref, ctrl_ref, sens_ref, *scratch
+    steps, sens_in, node_in, ctrl_in, out_ref, node_ref, ctrl_ref, sens_ref, *scratch
 ):
     node_xyz, ctrl_xyz, node_rows, ctrl_rows, done = scratch
     copies = [
@@ -75,15 +76,21 @@
     ]
     for copy in copies:
         copy.start()
-    copies[0].wait()
+    node_ref[...] = jnp.zeros_like(node_ref)
+    ctrl_ref[...] = jnp.zeros_like(ctrl_ref)
+    for copy in copies:
+        copy.wait()
     write_features(node_xyz, node_rows, True)
-    node_ref[...] = node_rows[...].T.astype(jnp.bfloat16)
-    copies[1].wait()
+    node_ref[:, 0:used] = node_rows[...].T.astype(jnp.bfloat16)
     write_features(ctrl_xyz, ctrl_rows, False)
-    ctrl_ref[...] = ctrl_rows[...].astype(jnp.bfloat16)
-    copies[2].wait()
-    block = (1 - lax.axis_index("core")) * 4 + lax.bitwise_xor(lax.axis_index("x"), by)
-    out_ref[...] = pulled_block(node_ref, ctrl_ref, sens_ref, block)
+    ctrl_ref[0:used, :] = ctrl_rows[...].astype(jnp.bfloat16)
+    core = lax.axis_index("core")
+    x = lax.axis_index("x")
+    for j, step in enumerate(steps):
+        block = (1 - core) * 4 + lax.bitwise_xor(x, step)
+        out_ref[:, j * span : (j + 1) * span] = pulled_block(
+            node_ref, ctrl_ref, sens_ref, block
+        )
 
 
 def pull_cost(nodes, blocks):
@@ -94,13 +101,13 @@
     )
 
 
-def first_pull(by, sens, node_xyz, ctrl_xyz):
+def first_pull(steps, sens, node_xyz, ctrl_xyz):
     rows, nodes = sens.shape
     ctrls = ctrl_xyz.shape[1]
     return pl.pallas_call(
-        functools.partial(first_kernel, by),
+        functools.partial(first_kernel, steps),
         out_shape=[
-            jax.ShapeDtypeStruct((rows, span), jnp.float32),
+            jax.ShapeDtypeStruct((rows, len(steps) * span), jnp.float32),
             jax.ShapeDtypeStruct((nodes, depth), jnp.bfloat16),
             jax.ShapeDtypeStruct((depth, ctrls), jnp.bfloat16),
             jax.ShapeDtypeStruct(sens.shape, sens.dtype),
@@ -110,47 +117,35 @@
         scratch_shapes=[
             pltpu.VMEM(node_xyz.shape, jnp.float32),
             pltpu.VMEM(ctrl_xyz.shape, jnp.float32),
-            pltpu.VMEM((depth, nodes), jnp.float32),
-            pltpu.VMEM((depth, ctrls), jnp.float32),
+            pltpu.VMEM((used, nodes), jnp.float32),
+            pltpu.VMEM((used, ctrls), jnp.float32),
             pltpu.SemaphoreType.DMA((3,)),
         ],
-        cost_estimate=pull_cost(nodes, 2),
+        cost_estimate=pull_cost(nodes, len(steps)),
         compiler_params=params,
         name="first_pull",
     )(*(pltpu.with_memory_space_constraint(a, pltpu.HBM) for a in (sens, node_xyz, ctrl_xyz)))
 
 
-def pull_kernel(other, steps, add_at, node_ref, ctrl_ref, sens_ref, *rest):
-    out_ref = rest[-1]
+def pull_kernel(other, step, add_at, node_ref, ctrl_ref, sens_ref, *rest):
     core = lax.axis_index("core")
-    x = lax.axis_index("x")
     half = (1 - core) if other else core
-    if len(steps) == 1:
-        block = half * 4 + lax.bitwise_xor(x, steps[0])
-        total = pulled_block(node_ref, ctrl_ref, sens_ref, block)
-        if len(rest) == 2:
-            total = total + rest[0][:, add_at * span : (add_at + 1) * span]
-        out_ref[...] = total
-        return
-
-    def body(j, carry):
-        block = half * 4 + lax.bitwise_xor(x, steps[0] + j * (steps[1] - steps[0]))
-        columns = pl.ds(pl.multiple_of(j * span, span), span)
-        out_ref[:, columns] = pulled_block(node_ref, ctrl_ref, sens_ref, block)
-        return carry
-
-    lax.fori_loop(0, len(steps), body, 0)
-
-
-def pull(prepared, other, steps, add=None, add_at=0):
+    block = half * 4 + lax.bitwise_xor(lax.axis_index("x"), step)
+    total = pulled_block(node_ref, ctrl_ref, sens_ref, block)
+    if len(rest) == 2:
+        total = total + rest[0][:, add_at * span : (add_at + 1) * span]
+    rest[-1][...] = total
+
+
+def pull(prepared, other, step, add=None, add_at=0):
     rows, nodes = prepared[2].shape
     args = list(prepared) + ([] if add is None else [add])
     return pl.pallas_call(
-        functools.partial(pull_kernel, other, steps, add_at),
-        out_shape=jax.ShapeDtypeStruct((rows, len(steps) * span), jnp.float32),
+        functools.partial(pull_kernel, other, step, add_at),
+        out_shape=jax.ShapeDtypeStruct((rows, span), jnp.float32),
         in_specs=[whole] * len(args),
         out_specs=whole,
-        cost_estimate=pull_cost(nodes, len(steps)),
+        cost_estimate=pull_cost(nodes, 1),
         compiler_params=params,
         name="pull",
     )(*args)
@@ -226,16 +221,17 @@
     def pulled(*args):
         return pull(prepared, *args)
 
-    first, *prepared = first_pull(2, sensitivity, node_xyz, ctrl_xyz)
-    first = swapped(first, "core", 1)
-    second = swapped(pulled(True, (1, 3)), "core", 1)
+    steps = (2, 1, 3)
+    shared, *prepared = first_pull(steps, sensitivity, node_xyz, ctrl_xyz)
+    shared = swapped(shared, "core", 1)
+    far = pulled(False, 2) + shared[:, :span]
     parts = [
-        swapped(pulled(False, (2,), first), "x", 2),
-        swapped(pulled(False, (1,), second, 0), "x", 1),
-        swapped(pulled(False, (3,), second, 1), "x", 3),
-        swapped(pulled(True, (0,)), "core", 1),
+        swapped(far, "x", 2),
+        swapped(pulled(False, 1, shared, 1), "x", 1),
+        swapped(pulled(False, 3, shared, 2), "x", 3),
+        swapped(pulled(True, 0), "core", 1),
     ]
-    summed = pulled(False, (0,))
+    summed = pulled(False, 0)
     for part in parts:
         summed = summed + part
 

time: 61 us -> 60.7 us (level)
    ppermute x13 -> x12, waiting for transfers between devices: 9.62 us -> 9.32 us  [swapped(): return lax.ppermute(value, axis, [(i, i ^ by) for i in range(size)])]
    pallas_call x7 -> x6, Pallas kernels: 16 us -> 15.8 us  [the longest x5 9.06 us: pull(): pl.pallas_call(functools.partial(pull_kernel, other, step, add_at), out_s...]
    ppermute x13 -> x12, starting transfers between devices: 23.9 us -> 23.9 us  [swapped(): return lax.ppermute(value, axis, [(i, i ^ by) for i in range(size)])]
  transfers between devices with their start and end apart: 13 -> 12, of which waited for: 7 -> 7; matrix products, arithmetic and copies ran while one was open for 0% -> 0% of each run, Pallas kernels for 15% -> 15%
where the time goes in v1:
time: 60.7 us; the launch traced here: 60.3 us
  starting transfers between devices  23.9 us (39%)
  Pallas kernels  17.2 us (28%)
  blocking collectives  9.75 us (16%)
  waiting for transfers between devices  9.32 us (15%)
    ppermute x12, starting transfers between devices, swapped(): return lax.ppermute(value, axis, [(i, i ^ by) for i in range(size)])  23.9 us
    all_to_all x1, blocking collectives, per_device(): lax.all_to_all(shares, ('y', 'zl'), split_axis=0, concat_axis=0, tiled=True)  9.75 us
    ppermute x12, waiting for transfers between devices, swapped(): return lax.ppermute(value, axis, [(i, i ^ by) for i in range(size)])  9.32 us
    pallas_call x5, Pallas kernels, pull(): pl.pallas_call(functools.partial(pull_kernel, other, step, add_at), out_s...  9.06 us
    pallas_call x1, Pallas kernels, first_pull(): pl.pallas_call(functools.partial(first_kernel, steps), out_shape=[jax.Sha...  6.77 us
  transfers between devices with their start and end apart: 12, of which 7 were waited for; matrix products, arithmetic and copies ran while one was open for 0% of the time, Pallas kernels for 15%

profile of v1, /device:TPU:1, one launch (start us, length us, event | category | flops | bytes accessed | tf_op | source)
XLA Modules:
  0.0 60.3 jit_solution(5613682831442281963)
XLA Ops:
  0.0 6.8 %first_pull.1 = (f32[96,768]{1,0:T(8,128)S(1)}, bf16[4096,128]{1,0:T(8,128)(2,1)S(1)}, bf16[128,2048]{1,0:T(8,128)(2,1)S(1)}, bf16[96,4096]{1,0:T(8,128)(2,1)S(1)}) custom-call(bf16[96,4096]{1,0:T(8,128)(2,1)} %sens_in.1, f32[3,4096]{1,0:T(4,128)} %node_in.1, f32[3,2048]{1,0:T(4,128)} %ctrl_in.1), custom_call_target="tpu_custom_call" | custom-call | flops 1258291200 | bytes 1835008 | tf_op jit(solution)/shard_map/first_pull/pallas_call | solution.py:107
  6.8 3.3 %collective-permute-start = (f32[96,768]{1,0:T(8,128)S(1)}, f32[96,768]{1,0:T(8,128)S(1)}, u32[]{:S(2)}, u32[]{:S(2)}) collective-permute-start(f32[96,768]{1,0:T(8,128)S(1)} %get-tuple-element.12), channel_id=1, source_target_pairs={{0,8},{8,0},{1,9},{9,1},{2,10},{10,2},{3,11},{11,3},{4,12},{12,4},... | collective-permute-start | bytes 884744 | tf_op jit(solution)/shard_map/ppermute | solution.py:217
  10.1 1.8 %pull.9 = f32[96,256]{1,0:T(8,128)S(1)} custom-call(bf16[4096,128]{1,0:T(8,128)(2,1)S(1)} %get-tuple-element.9.node_ref, bf16[128,2048]{1,0:T(8,128)(2,1)S(1)} %get-tuple-element.10.ctrl_ref, bf16[96,4096]{1,0:T(8,128)(2,1)S(1)} %get-tuple-element.11.sens_ref), custom_call_target="tpu_custom_call" | custom-call | flops 419430400 | bytes 1835008 | tf_op jit(solution)/shard_map/pull/pallas_call | solution.py:143
  12.0 1.8 %pull.6 = f32[96,256]{1,0:T(8,128)S(1)} custom-call(bf16[4096,128]{1,0:T(8,128)(2,1)S(1)} %get-tuple-element.9.node_ref, bf16[128,2048]{1,0:T(8,128)(2,1)S(1)} %get-tuple-element.10.ctrl_ref, bf16[96,4096]{1,0:T(8,128)(2,1)S(1)} %get-tuple-element.11.sens_ref), custom_call_target="tpu_custom_call" | custom-call | flops 419430400 | bytes 1835008 | tf_op jit(solution)/shard_map/pull/pallas_call | solution.py:143
  13.9 1.3 %collective-permute-start.1 = (f32[96,256]{1,0:T(8,128)S(1)}, f32[96,256]{1,0:T(8,128)S(1)}, u32[]{:S(2)}, u32[]{:S(2)}) collective-permute-start(f32[96,256]{1,0:T(8,128)S(1)} %slice_add_fusion), channel_id=1, source_target_pairs={{0,32},{16,48},{32,0},{48,16},{1,33},{17,49},{33,1},{49,17},{2,34}... | collective-permute-start | bytes 294920 | tf_op jit(solution)/shard_map/ppermute | solution.py:217
  15.1 1.8 %pull.7 = f32[96,256]{1,0:T(8,128)S(1)} custom-call(bf16[4096,128]{1,0:T(8,128)(2,1)S(1)} %get-tuple-element.9.node_ref, bf16[128,2048]{1,0:T(8,128)(2,1)S(1)} %get-tuple-element.10.ctrl_ref, bf16[96,4096]{1,0:T(8,128)(2,1)S(1)} %get-tuple-element.11.sens_ref, f32[96,768]{1,0:T(8,128)S(1)} %collective-permute-done.rest_0_), custom_call_target="tpu_custom_call" | custom-call | flops 419430400 | bytes 1835008 | tf_op jit(solution)/shard_map/pull/pallas_call | solution.py:143
  17.4 1.8 %pull.8 = f32[96,256]{1,0:T(8,128)S(1)} custom-call(bf16[4096,128]{1,0:T(8,128)(2,1)S(1)} %get-tuple-element.9.node_ref, bf16[128,2048]{1,0:T(8,128)(2,1)S(1)} %get-tuple-element.10.ctrl_ref, bf16[96,4096]{1,0:T(8,128)(2,1)S(1)} %get-tuple-element.11.sens_ref, f32[96,768]{1,0:T(8,128)S(1)} %collective-permute-done.rest_0_), custom_call_target="tpu_custom_call" | custom-call | flops 419430400 | bytes 1835008 | tf_op jit(solution)/shard_map/pull/pallas_call | solution.py:143
  19.2 2.0 %collective-permute-start.3 = (f32[96,256]{1,0:T(8,128)S(1)}, f32[96,256]{1,0:T(8,128)S(1)}, u32[]{:S(2)}, u32[]{:S(2)}) collective-permute-start(f32[96,256]{1,0:T(8,128)S(1)} %pull.8), channel_id=1, source_target_pairs={{0,48},{16,32},{32,16},{48,0},{1,49},{17,33},{33,17},{49,1},{2,50}... | collective-permute-start | bytes 294920 | tf_op jit(solution)/shard_map/ppermute | solution.py:217
  21.2 1.8 %pull.5 = f32[96,256]{1,0:T(8,128)S(1)} custom-call(bf16[4096,128]{1,0:T(8,128)(2,1)S(1)} %get-tuple-element.9.node_ref, bf16[128,2048]{1,0:T(8,128)(2,1)S(1)} %get-tuple-element.10.ctrl_ref, bf16[96,4096]{1,0:T(8,128)(2,1)S(1)} %get-tuple-element.11.sens_ref), custom_call_target="tpu_custom_call" | custom-call | flops 419430400 | bytes 1835008 | tf_op jit(solution)/shard_map/pull/pallas_call | solution.py:143
  23.0 0.9 %collective-permute-done.3 = f32[96,256]{1,0:T(8,128)S(1)} collective-permute-done((f32[96,256]{1,0:T(8,128)S(1)}, f32[96,256]{1,0:T(8,128)S(1)}, u32[]{:S(2)}, u32[]{:S(2)}) %collective-permute-start.3) | collective-permute-done | bytes 98336 | tf_op jit(solution)/shard_map/ppermute | solution.py:217
  24.0 7.0 %collective-permute-start.5 = (bf16[96,256]{1,0:T(8,128)(2,1)S(1)}, bf16[96,256]{1,0:T(8,128)(2,1)S(1)}, u32[]{:S(2)}, u32[]{:S(2)}) collective-permute-start(bf16[96,256]{1,0:T(8,128)(2,1)S(1)} %get-tuple-element.13), channel_id=1, source_target_pairs={{0,128},{64,192},{128,0},{192,64},{1,129},{65,193},{129,1},{193,65... | collective-permute-start | bytes 147464 | tf_op jit(solution)/shard_map/ppermute | solution.py:217
  31.0 1.2 %collective-permute-start.6 = (bf16[96,256]{1,0:T(8,128)(2,1)S(1)}, bf16[96,256]{1,0:T(8,128)(2,1)S(1)}, u32[]{:S(2)}, u32[]{:S(2)}) collective-permute-start(bf16[96,256]{1,0:T(8,128)(2,1)S(1)} %get-tuple-element.13), channel_id=1, source_target_pairs={{0,64},{64,0},{128,192},{192,128},{1,65},{65,1},{129,193},{193,129... | collective-permute-start | bytes 147464 | tf_op jit(solution)/shard_map/ppermute | solution.py:217
  32.5 2.7 %collective-permute-done.6 = bf16[96,256]{1,0:T(8,128)(2,1)S(1)} collective-permute-done((bf16[96,256]{1,0:T(8,128)(2,1)S(1)}, bf16[96,256]{1,0:T(8,128)(2,1)S(1)}, u32[]{:S(2)}, u32[]{:S(2)}) %collective-permute-start.6) | collective-permute-done | bytes 49184 | tf_op jit(solution)/shard_map/ppermute | solution.py:217
  35.1 2.2 %collective-permute-done.7 = bf16[96,256]{1,0:T(8,128)(2,1)S(1)} collective-permute-done((bf16[96,256]{1,0:T(8,128)(2,1)S(1)}, bf16[96,256]{1,0:T(8,128)(2,1)S(1)}, u32[]{:S(2)}, u32[]{:S(2)}) %collective-permute-start.7) | collective-permute-done | bytes 49184 | tf_op jit(solution)/shard_map/ppermute | solution.py:217
  37.4 1.1 %collective-permute-start.10 = (bf16[96,256]{1,0:T(8,128)(2,1)S(1)}, bf16[96,256]{1,0:T(8,128)(2,1)S(1)}, u32[]{:S(2)}, u32[]{:S(2)}) collective-permute-start(bf16[96,256]{1,0:T(8,128)(2,1)S(1)} %add_convert_fusion.refs_0_), channel_id=1, source_target_pairs={{0,48},{16,32},{32,16},{48,0},{1,49},{17,33},{33,17},{49,1},{2,50}... | collective-permute-start | bytes 147464 | tf_op jit(solution)/shard_map/ppermute | solution.py:217
  38.4 0.7 %collective-permute-start.8 = (bf16[96,256]{1,0:T(8,128)(2,1)S(1)}, bf16[96,256]{1,0:T(8,128)(2,1)S(1)}, u32[]{:S(2)}, u32[]{:S(2)}) collective-permute-start(bf16[96,256]{1,0:T(8,128)(2,1)S(1)} %add_convert_fusion.refs_0_), channel_id=1, source_target_pairs={{0,32},{16,48},{32,0},{48,16},{1,33},{17,49},{33,1},{49,17},{2,34}... | collective-permute-start | bytes 147464 | tf_op jit(solution)/shard_map/ppermute | solution.py:217
  39.2 1.5 %collective-permute-start.9 = (bf16[96,256]{1,0:T(8,128)(2,1)S(1)}, bf16[96,256]{1,0:T(8,128)(2,1)S(1)}, u32[]{:S(2)}, u32[]{:S(2)}) collective-permute-start(bf16[96,256]{1,0:T(8,128)(2,1)S(1)} %add_convert_fusion.refs_0_), channel_id=1, source_target_pairs={{0,16},{16,0},{32,48},{48,32},{1,17},{17,1},{33,49},{49,33},{2,18}... | collective-permute-start | bytes 147464 | tf_op jit(solution)/shard_map/ppermute | solution.py:217
  40.7 0.9 %collective-permute-done.10.refs_3_ = bf16[96,256]{1,0:T(8,128)(2,1)S(1)} collective-permute-done((bf16[96,256]{1,0:T(8,128)(2,1)S(1)}, bf16[96,256]{1,0:T(8,128)(2,1)S(1)}, u32[]{:S(2)}, u32[]{:S(2)}) %collective-permute-start.10) | collective-permute-done | bytes 49184 | tf_op jit(solution)/shard_map/ppermute | solution.py:217
  41.6 1.3 %collective-permute-done.8.refs_1_ = bf16[96,256]{1,0:T(8,128)(2,1)S(1)} collective-permute-done((bf16[96,256]{1,0:T(8,128)(2,1)S(1)}, bf16[96,256]{1,0:T(8,128)(2,1)S(1)}, u32[]{:S(2)}, u32[]{:S(2)}) %collective-permute-start.8) | collective-permute-done | bytes 49184 | tf_op jit(solution)/shard_map/ppermute | solution.py:217
  42.9 5.2 %collective-permute-start.11 = (bf16[96,1024]{1,0:T(8,128)(2,1)S(1)}, bf16[96,1024]{1,0:T(8,128)(2,1)S(1)}, u32[]{:S(2)}, u32[]{:S(2)}) collective-permute-start(bf16[96,1024]{1,0:T(8,128)(2,1)S(1)} %pad_maximum_fusion), channel_id=1, source_target_pairs={{0,8},{8,0},{1,9},{9,1},{2,10},{10,2},{3,11},{11,3},{4,12},{12,4},... | collective-permute-start | bytes 589832 | tf_op jit(solution)/shard_map/ppermute | solution.py:217
  48.1 1.1 %collective-permute-done.11.refs_4_ = bf16[96,1024]{1,0:T(8,128)(2,1)S(1)} collective-permute-done((bf16[96,1024]{1,0:T(8,128)(2,1)S(1)}, bf16[96,1024]{1,0:T(8,128)(2,1)S(1)}, u32[]{:S(2)}, u32[]{:S(2)}) %collective-permute-start.11) | collective-permute-done | bytes 196640 | tf_op jit(solution)/shard_map/ppermute | solution.py:217
  49.2 0.5 product.1
  49.8 9.8 %all_to_all.5.shares_ref = bf16[8,48,128]{2,1,0:T(8,128)(2,1)S(1)} all-to-all(bf16[8,48,128]{2,1,0:T(8,128)(2,1)S(1)} %product.1), channel_id=1, replica_groups=mesh['zh'=4,'x'=4,'core'=2,'y'=4,'zl'=2] {'y','zl'}, dimensions={0} | all-to-all | bytes 196608 | tf_op jit(solution)/shard_map/all_to_all | solution.py:247
  59.5 0.8 %finish.1 = f32[64,96]{1,0:T(8,128)} custom-call(bf16[8,48,128]{2,1,0:T(8,128)(2,1)S(1)} %all_to_all.5.shares_ref), custom_call_target="tpu_custom_call" | custom-call | tf_op jit(solution)/shard_map/finish/pallas_call | solution.py:205
  (15 shorter events, 0.9 us)
Async XLA Ops:
  6.8 7.0 %collective-permute-start = (f32[96,768]{1,0:T(8,128)S(1)}, f32[96,768]{1,0:T(8,128)S(1)}, u32[]{:S(2)}, u32[]{:S(2)}) collective-permute-start(f32[96,768]{1,0:T(8,128)S(1)} %get-tuple-element.12), channel_id=1, source_target_pairs={{0,8},{8,0},{1,9},{9,1},{2,10},{10,2},{3,11},{11,3},{4,12},{12,4},... | collective-permute-start | bytes 884744 | tf_op jit(solution)/shard_map/ppermute | solution.py:217
  11.9 11.1 %collective-permute-start.4 = (f32[96,256]{1,0:T(8,128)S(1)}, f32[96,256]{1,0:T(8,128)S(1)}, u32[]{:S(2)}, u32[]{:S(2)}) collective-permute-start(f32[96,256]{1,0:T(8,128)S(1)} %pull.9), channel_id=1, source_target_pairs={{0,8},{8,0},{1,9},{9,1},{2,10},{10,2},{3,11},{11,3},{4,12},{12,4},... | collective-permute-start | bytes 294920 | tf_op jit(solution)/shard_map/ppermute | solution.py:217
  13.9 9.2 %collective-permute-start.1 = (f32[96,256]{1,0:T(8,128)S(1)}, f32[96,256]{1,0:T(8,128)S(1)}, u32[]{:S(2)}, u32[]{:S(2)}) collective-permute-start(f32[96,256]{1,0:T(8,128)S(1)} %slice_add_fusion), channel_id=1, source_target_pairs={{0,32},{16,48},{32,0},{48,16},{1,33},{17,49},{33,1},{49,17},{2,34}... | collective-permute-start | bytes 294920 | tf_op jit(solution)/shard_map/ppermute | solution.py:217
  17.0 6.1 %collective-permute-start.2 = (f32[96,256]{1,0:T(8,128)S(1)}, f32[96,256]{1,0:T(8,128)S(1)}, u32[]{:S(2)}, u32[]{:S(2)}) collective-permute-start(f32[96,256]{1,0:T(8,128)S(1)} %pull.7), channel_id=1, source_target_pairs={{0,16},{16,0},{32,48},{48,32},{1,17},{17,1},{33,49},{49,33},{2,18}... | collective-permute-start | bytes 294920 | tf_op jit(solution)/shard_map/ppermute | solution.py:217
  19.2 30.0 %copy-start = (bf16[2048,512]{1,0:T(8,128)(2,1)S(1)}, bf16[2048,512]{1,0:T(8,128)(2,1)}, u32[]{:S(2)}) copy-start(bf16[2048,512]{1,0:T(8,128)(2,1)} %refs_5_.1) | copy-start | bytes 6291460
  19.2 4.8 %collective-permute-start.3 = (f32[96,256]{1,0:T(8,128)S(1)}, f32[96,256]{1,0:T(8,128)S(1)}, u32[]{:S(2)}, u32[]{:S(2)}) collective-permute-start(f32[96,256]{1,0:T(8,128)S(1)} %pull.8), channel_id=1, source_target_pairs={{0,48},{16,32},{32,16},{48,0},{1,49},{17,33},{33,17},{49,1},{2,50}... | collective-permute-start | bytes 294920 | tf_op jit(solution)/shard_map/ppermute | solution.py:217
  24.0 8.5 %collective-permute-start.5 = (bf16[96,256]{1,0:T(8,128)(2,1)S(1)}, bf16[96,256]{1,0:T(8,128)(2,1)S(1)}, u32[]{:S(2)}, u32[]{:S(2)}) collective-permute-start(bf16[96,256]{1,0:T(8,128)(2,1)S(1)} %get-tuple-element.13), channel_id=1, source_target_pairs={{0,128},{64,192},{128,0},{192,64},{1,129},{65,193},{129,1},{193,65... | collective-permute-start | bytes 147464 | tf_op jit(solution)/shard_map/ppermute | solution.py:217
  31.0 4.1 %collective-permute-start.6 = (bf16[96,256]{1,0:T(8,128)(2,1)S(1)}, bf16[96,256]{1,0:T(8,128)(2,1)S(1)}, u32[]{:S(2)}, u32[]{:S(2)}) collective-permute-start(bf16[96,256]{1,0:T(8,128)(2,1)S(1)} %get-tuple-element.13), channel_id=1, source_target_pairs={{0,64},{64,0},{128,192},{192,128},{1,65},{65,1},{129,193},{193,129... | collective-permute-start | bytes 147464 | tf_op jit(solution)/shard_map/ppermute | solution.py:217
  32.2 5.1 %collective-permute-start.7 = (bf16[96,256]{1,0:T(8,128)(2,1)S(1)}, bf16[96,256]{1,0:T(8,128)(2,1)S(1)}, u32[]{:S(2)}, u32[]{:S(2)}) collective-permute-start(bf16[96,256]{1,0:T(8,128)(2,1)S(1)} %get-tuple-element.13), channel_id=1, source_target_pairs={{0,192},{64,128},{128,64},{192,0},{1,193},{65,129},{129,65},{193,1... | collective-permute-start | bytes 147464 | tf_op jit(solution)/shard_map/ppermute | solution.py:217
  37.4 4.2 %collective-permute-start.10 = (bf16[96,256]{1,0:T(8,128)(2,1)S(1)}, bf16[96,256]{1,0:T(8,128)(2,1)S(1)}, u32[]{:S(2)}, u32[]{:S(2)}) collective-permute-start(bf16[96,256]{1,0:T(8,128)(2,1)S(1)} %add_convert_fusion.refs_0_), channel_id=1, source_target_pairs={{0,48},{16,32},{32,16},{48,0},{1,49},{17,33},{33,17},{49,1},{2,50}... | collective-permute-start | bytes 147464 | tf_op jit(solution)/shard_map/ppermute | solution.py:217
  38.4 4.4 %collective-permute-start.8 = (bf16[96,256]{1,0:T(8,128)(2,1)S(1)}, bf16[96,256]{1,0:T(8,128)(2,1)S(1)}, u32[]{:S(2)}, u32[]{:S(2)}) collective-permute-start(bf16[96,256]{1,0:T(8,128)(2,1)S(1)} %add_convert_fusion.refs_0_), channel_id=1, source_target_pairs={{0,32},{16,48},{32,0},{48,16},{1,33},{17,49},{33,1},{49,17},{2,34}... | collective-permute-start | bytes 147464 | tf_op jit(solution)/shard_map/ppermute | solution.py:217
  39.2 3.7 %collective-permute-start.9 = (bf16[96,256]{1,0:T(8,128)(2,1)S(1)}, bf16[96,256]{1,0:T(8,128)(2,1)S(1)}, u32[]{:S(2)}, u32[]{:S(2)}) collective-permute-start(bf16[96,256]{1,0:T(8,128)(2,1)S(1)} %add_convert_fusion.refs_0_), channel_id=1, source_target_pairs={{0,16},{16,0},{32,48},{48,32},{1,17},{17,1},{33,49},{49,33},{2,18}... | collective-permute-start | bytes 147464 | tf_op jit(solution)/shard_map/ppermute | solution.py:217
  42.9 6.3 %collective-permute-start.11 = (bf16[96,1024]{1,0:T(8,128)(2,1)S(1)}, bf16[96,1024]{1,0:T(8,128)(2,1)S(1)}, u32[]{:S(2)}, u32[]{:S(2)}) collective-permute-start(bf16[96,1024]{1,0:T(8,128)(2,1)S(1)} %pad_maximum_fusion), channel_id=1, source_target_pairs={{0,8},{8,0},{1,9},{9,1},{2,10},{10,2},{3,11},{11,3},{4,12},{12,4},... | collective-permute-start | bytes 589832 | tf_op jit(solution)/shard_map/ppermute | solution.py:217

commit v2 on v1

--- a/solution.py
+++ b/solution.py
@@ -64,8 +64,12 @@
     return total * (1.0 / 256.0)
 
 
+def block_of(step):
+    return lax.axis_index("core") * 4 + lax.bitwise_xor(lax.axis_index("x"), step)
+
+
 def first_kernel(
-    steps, sens_in, node_in, ctrl_in, out_ref, node_ref, ctrl_ref, sens_ref, *scratch
+    step, sens_in, node_in, ctrl_in, out_ref, node_ref, sens_ref, ctrl_ref, *scratch
 ):
     node_xyz, ctrl_xyz, node_rows, ctrl_rows, done = scratch
     copies = [
@@ -84,13 +88,7 @@
     node_ref[:, 0:used] = node_rows[...].T.astype(jnp.bfloat16)
     write_features(ctrl_xyz, ctrl_rows, False)
     ctrl_ref[0:used, :] = ctrl_rows[...].astype(jnp.bfloat16)
-    core = lax.axis_index("core")
-    x = lax.axis_index("x")
-    for j, step in enumerate(steps):
-        block = (1 - core) * 4 + lax.bitwise_xor(x, step)
-        out_ref[:, j * span : (j + 1) * span] = pulled_block(
-            node_ref, ctrl_ref, sens_ref, block
-        )
+    out_ref[...] = pulled_block(node_ref, ctrl_ref, sens_ref, block_of(step))
 
 
 def pull_cost(nodes, blocks):
@@ -101,16 +99,16 @@
     )
 
 
-def first_pull(steps, sens, node_xyz, ctrl_xyz):
+def first_pull(step, sens, node_xyz, ctrl_xyz):
     rows, nodes = sens.shape
     ctrls = ctrl_xyz.shape[1]
     return pl.pallas_call(
-        functools.partial(first_kernel, steps),
+        functools.partial(first_kernel, step),
         out_shape=[
-            jax.ShapeDtypeStruct((rows, len(steps) * span), jnp.float32),
+            jax.ShapeDtypeStruct((rows, span), jnp.float32),
             jax.ShapeDtypeStruct((nodes, depth), jnp.bfloat16),
+            jax.ShapeDtypeStruct(sens.shape, sens.dtype),
             jax.ShapeDtypeStruct((depth, ctrls), jnp.bfloat16),
-            jax.ShapeDtypeStruct(sens.shape, sens.dtype),
         ],
         in_specs=[pl.BlockSpec(memory_space=pltpu.HBM)] * 3,
         out_specs=[whole] * 4,
@@ -121,34 +119,56 @@
             pltpu.VMEM((used, ctrls), jnp.float32),
             pltpu.SemaphoreType.DMA((3,)),
         ],
-        cost_estimate=pull_cost(nodes, len(steps)),
+        cost_estimate=pull_cost(nodes, 1),
         compiler_params=params,
         name="first_pull",
     )(*(pltpu.with_memory_space_constraint(a, pltpu.HBM) for a in (sens, node_xyz, ctrl_xyz)))
 
 
-def pull_kernel(other, step, add_at, node_ref, ctrl_ref, sens_ref, *rest):
-    core = lax.axis_index("core")
-    half = (1 - core) if other else core
-    block = half * 4 + lax.bitwise_xor(lax.axis_index("x"), step)
-    total = pulled_block(node_ref, ctrl_ref, sens_ref, block)
-    if len(rest) == 2:
-        total = total + rest[0][:, add_at * span : (add_at + 1) * span]
-    rest[-1][...] = total
-
-
-def pull(prepared, other, step, add=None, add_at=0):
-    rows, nodes = prepared[2].shape
-    args = list(prepared) + ([] if add is None else [add])
-    return pl.pallas_call(
-        functools.partial(pull_kernel, other, step, add_at),
+def second_kernel(
+    step, part_ref, node_xyz, sens_ref, ctrl_ref, out_ref, node_ref, node_rows
+):
+    node_ref[...] = jnp.zeros_like(node_ref)
+    write_features(node_xyz, node_rows, True)
+    node_ref[:, 0:used] = node_rows[...].T.astype(jnp.bfloat16)
+    total = pulled_block(node_ref, ctrl_ref, sens_ref, block_of(step))
+    out_ref[...] = total + part_ref[...]
+
+
+def second_pull(step, part, node_xyz, sens, ctrl_feat):
+    rows, nodes = sens.shape
+    return pl.pallas_call(
+        functools.partial(second_kernel, step),
+        out_shape=[
+            jax.ShapeDtypeStruct((rows, span), jnp.float32),
+            jax.ShapeDtypeStruct((nodes, depth), jnp.bfloat16),
+        ],
+        in_specs=[whole] * 4,
+        out_specs=[whole] * 2,
+        scratch_shapes=[pltpu.VMEM((used, nodes), jnp.float32)],
+        cost_estimate=pull_cost(nodes, 1),
+        compiler_params=params,
+        name="second_pull",
+    )(part, node_xyz, sens, ctrl_feat)
+
+
+def pull_kernel(step, node_a, sens_a, node_b, sens_b, ctrl_ref, out_ref):
+    block = block_of(step)
+    total = pulled_block(node_a, ctrl_ref, sens_a, block)
+    out_ref[...] = total + pulled_block(node_b, ctrl_ref, sens_b, block)
+
+
+def pull(step, *prepared):
+    rows, nodes = prepared[1].shape
+    return pl.pallas_call(
+        functools.partial(pull_kernel, step),
         out_shape=jax.ShapeDtypeStruct((rows, span), jnp.float32),
-        in_specs=[whole] * len(args),
+        in_specs=[whole] * len(prepared),
         out_specs=whole,
-        cost_estimate=pull_cost(nodes, 1),
+        cost_estimate=pull_cost(nodes, 2),
         compiler_params=params,
         name="pull",
-    )(*args)
+    )(*prepared)
 
 
 def product_kernel(order, *refs):
@@ -218,20 +238,18 @@
 
 
 def per_device(sensitivity, node_xyz, ctrl_xyz, inverse):
-    def pulled(*args):
-        return pull(prepared, *args)
-
-    steps = (2, 1, 3)
-    shared, *prepared = first_pull(steps, sensitivity, node_xyz, ctrl_xyz)
-    shared = swapped(shared, "core", 1)
-    far = pulled(False, 2) + shared[:, :span]
-    parts = [
-        swapped(far, "x", 2),
-        swapped(pulled(False, 1, shared, 1), "x", 1),
-        swapped(pulled(False, 3, shared, 2), "x", 3),
-        swapped(pulled(True, 0), "core", 1),
-    ]
-    summed = pulled(False, 0)
+    other_sens = swapped(sensitivity, "core", 1)
+    other_xyz = swapped(node_xyz, "core", 1)
+    far, node_feat, sens, ctrl_feat = first_pull(
+        2, sensitivity, node_xyz, ctrl_xyz
+    )
+    far, other_feat = second_pull(2, far, other_xyz, other_sens, ctrl_feat)
+    prepared = (node_feat, sens, other_feat, other_sens, ctrl_feat)
+    parts = [swapped(far, "x", 2)]
+    for step in (1, 3):
+        block = pull(step, *prepared)
+        parts.append(swapped(block, "x", step))
+    summed = pull(0, *prepared)
     for part in parts:
         summed = summed + part
 

time: 60.7 us -> 61.5 us (1.013)
    pallas_call x6 -> x5, Pallas kernels: 15.8 us -> 16.2 us  [the longest x3 10.2 us: pull(): pl.pallas_call(functools.partial(pull_kernel, step), out_shape=jax.ShapeD...]
  transfers between devices with their start and end apart: 12 -> 12, of which waited for: 7 -> 5; matrix products, arithmetic and copies ran while one was open for 0% -> 0% of each run, Pallas kernels for 15% -> 17%
where the time goes in v2:
time: 61.5 us; the launch traced here: 60.6 us
  starting transfers between devices  23.7 us (39%)
  Pallas kernels  17.5 us (28%)
  blocking collectives  9.77 us (16%)
  waiting for transfers between devices  9.37 us (15%)
    ppermute x12, starting transfers between devices, swapped(): return lax.ppermute(value, axis, [(i, i ^ by) for i in range(size)])  23.7 us
    pallas_call x3, Pallas kernels, pull(): pl.pallas_call(functools.partial(pull_kernel, step), out_shape=jax.ShapeD...  10.2 us
    all_to_all x1, blocking collectives, per_device(): lax.all_to_all(shares, ('y', 'zl'), split_axis=0, concat_axis=0, tiled=True)  9.77 us
    ppermute x12, waiting for transfers between devices, swapped(): return lax.ppermute(value, axis, [(i, i ^ by) for i in range(size)])  9.37 us
    pallas_call x1, Pallas kernels, first_pull(): pl.pallas_call(functools.partial(first_kernel, step), out_shape=[jax.Shap...  3.61 us
    pallas_call x1, Pallas kernels, second_pull(): pl.pallas_call(functools.partial(second_kernel, step), out_shape=[jax.Sha...  2.39 us
  transfers between devices with their start and end apart: 12, of which 5 were waited for; matrix products, arithmetic and copies ran while one was open for 0% of the time, Pallas kernels for 17%

profile of v2, /device:TPU:1, one launch (start us, length us, event | category | flops | bytes accessed | tf_op | source)
XLA Modules:
  0.0 60.6 jit_solution(851488877907760866)
XLA Ops:
  0.0 3.2 %collective-permute-start.1 = (bf16[96,4096]{1,0:T(8,128)(2,1)}, bf16[96,4096]{1,0:T(8,128)(2,1)S(1)}, u32[]{:S(2)}, u32[]{:S(2)}) collective-permute-start(bf16[96,4096]{1,0:T(8,128)(2,1)} %sens_in.1), channel_id=1, source_target_pairs={{0,8},{8,0},{1,9},{9,1},{2,10},{10,2},{3,11},{11,3},{4,12},{12,4},... | collective-permute-start | bytes 2359304 | tf_op jit(solution)/shard_map/ppermute | solution.py:237
  3.2 0.0 collective-permute-start
  3.2 3.6 %first_pull.1 = (f32[96,256]{1,0:T(8,128)S(1)}, bf16[4096,128]{1,0:T(8,128)(2,1)S(1)}, bf16[96,4096]{1,0:T(8,128)(2,1)S(1)}, bf16[128,2048]{1,0:T(8,128)(2,1)S(1)}) custom-call(bf16[96,4096]{1,0:T(8,128)(2,1)} %sens_in.1, f32[3,4096]{1,0:T(4,128)} %node_in.1, f32[3,2048]{1,0:T(4,128)} %ctrl_in.1), custom_call_target="tpu_custom_call" | custom-call | flops 419430400 | bytes 1835008 | tf_op jit(solution)/shard_map/first_pull/pallas_call | solution.py:105
  6.8 2.4 %second_pull.1 = (f32[96,256]{1,0:T(8,128)S(1)}, bf16[4096,128]{1,0:T(8,128)(2,1)S(1)}) custom-call(f32[96,256]{1,0:T(8,128)S(1)} %get-tuple-element.13.part_ref, f32[3,4096]{1,0:T(4,128)S(1)} %collective-permute-done.node_xyz, bf16[96,4096]{1,0:T(8,128)(2,1)S(1)} %collective-permute-done.1.sens_ref.sens_b, bf16[128,2048]{1,0:T(8,128)(2,1)S(1)} %get-tuple-element.14.ctrl_ref), custom_call_target="tpu_custom_call" | custom-call | flops 419430400 | bytes 1835008 | tf_op jit(solution)/shard_map/second_pull/pallas_call | solution.py:140
  9.2 3.4 %pull.4 = f32[96,256]{1,0:T(8,128)S(1)} custom-call(bf16[4096,128]{1,0:T(8,128)(2,1)S(1)} %get-tuple-element.11.node_a, bf16[96,4096]{1,0:T(8,128)(2,1)S(1)} %get-tuple-element.12.sens_a, bf16[4096,128]{1,0:T(8,128)(2,1)S(1)} %get-tuple-element.15.node_b, bf16[96,4096]{1,0:T(8,128)(2,1)S(1)} %collective-permute-done.1.sens_ref.sens_b, ...), custom_call_target="tpu_custom_call" | custom-call | flops 838860800 | bytes 1835008 | tf_op jit(solution)/shard_map/pull/pallas_call | solution.py:163
  12.6 0.3 collective-permute-start.3
  12.9 3.4 %pull.5 = f32[96,256]{1,0:T(8,128)S(1)} custom-call(bf16[4096,128]{1,0:T(8,128)(2,1)S(1)} %get-tuple-element.11.node_a, bf16[96,4096]{1,0:T(8,128)(2,1)S(1)} %get-tuple-element.12.sens_a, bf16[4096,128]{1,0:T(8,128)(2,1)S(1)} %get-tuple-element.15.node_b, bf16[96,4096]{1,0:T(8,128)(2,1)S(1)} %collective-permute-done.1.sens_ref.sens_b, ...), custom_call_target="tpu_custom_call" | custom-call | flops 838860800 | bytes 1835008 | tf_op jit(solution)/shard_map/pull/pallas_call | solution.py:163
  16.3 1.4 %collective-permute-start.4 = (f32[96,256]{1,0:T(8,128)S(1)}, f32[96,256]{1,0:T(8,128)S(1)}, u32[]{:S(2)}, u32[]{:S(2)}) collective-permute-start(f32[96,256]{1,0:T(8,128)S(1)} %pull.5), channel_id=1, source_target_pairs={{0,48},{16,32},{32,16},{48,0},{1,49},{17,33},{33,17},{49,1},{2,50}... | collective-permute-start | bytes 294920 | tf_op jit(solution)/shard_map/ppermute | solution.py:237
  17.7 1.9 %collective-permute-start.2 = (f32[96,256]{1,0:T(8,128)S(1)}, f32[96,256]{1,0:T(8,128)S(1)}, u32[]{:S(2)}, u32[]{:S(2)}) collective-permute-start(f32[96,256]{1,0:T(8,128)S(1)} %get-tuple-element.16), channel_id=1, source_target_pairs={{0,32},{16,48},{32,0},{48,16},{1,33},{17,49},{33,1},{49,17},{2,34}... | collective-permute-start | bytes 294920 | tf_op jit(solution)/shard_map/ppermute | solution.py:237
  19.6 3.4 %pull.3 = f32[96,256]{1,0:T(8,128)S(1)} custom-call(bf16[4096,128]{1,0:T(8,128)(2,1)S(1)} %get-tuple-element.11.node_a, bf16[96,4096]{1,0:T(8,128)(2,1)S(1)} %get-tuple-element.12.sens_a, bf16[4096,128]{1,0:T(8,128)(2,1)S(1)} %get-tuple-element.15.node_b, bf16[96,4096]{1,0:T(8,128)(2,1)S(1)} %collective-permute-done.1.sens_ref.sens_b, ...), custom_call_target="tpu_custom_call" | custom-call | flops 838860800 | bytes 1835008 | tf_op jit(solution)/shard_map/pull/pallas_call | solution.py:163
  23.1 5.8 %collective-permute-start.7 = (bf16[96,256]{1,0:T(8,128)(2,1)S(1)}, bf16[96,256]{1,0:T(8,128)(2,1)S(1)}, u32[]{:S(2)}, u32[]{:S(2)}) collective-permute-start(bf16[96,256]{1,0:T(8,128)(2,1)S(1)} %get-tuple-element.17), channel_id=1, source_target_pairs={{0,192},{64,128},{128,64},{192,0},{1,193},{65,129},{129,65},{193,1... | collective-permute-start | bytes 147464 | tf_op jit(solution)/shard_map/ppermute | solution.py:237
  28.9 1.2 %collective-permute-start.6 = (bf16[96,256]{1,0:T(8,128)(2,1)S(1)}, bf16[96,256]{1,0:T(8,128)(2,1)S(1)}, u32[]{:S(2)}, u32[]{:S(2)}) collective-permute-start(bf16[96,256]{1,0:T(8,128)(2,1)S(1)} %get-tuple-element.17), channel_id=1, source_target_pairs={{0,64},{64,0},{128,192},{192,128},{1,65},{65,1},{129,193},{193,129... | collective-permute-start | bytes 147464 | tf_op jit(solution)/shard_map/ppermute | solution.py:237
  30.1 1.0 %collective-permute-start.5 = (bf16[96,256]{1,0:T(8,128)(2,1)S(1)}, bf16[96,256]{1,0:T(8,128)(2,1)S(1)}, u32[]{:S(2)}, u32[]{:S(2)}) collective-permute-start(bf16[96,256]{1,0:T(8,128)(2,1)S(1)} %get-tuple-element.17), channel_id=1, source_target_pairs={{0,128},{64,192},{128,0},{192,64},{1,129},{65,193},{129,1},{193,65... | collective-permute-start | bytes 147464 | tf_op jit(solution)/shard_map/ppermute | solution.py:237
  31.1 1.9 %collective-permute-done.6 = bf16[96,256]{1,0:T(8,128)(2,1)S(1)} collective-permute-done((bf16[96,256]{1,0:T(8,128)(2,1)S(1)}, bf16[96,256]{1,0:T(8,128)(2,1)S(1)}, u32[]{:S(2)}, u32[]{:S(2)}) %collective-permute-start.6) | collective-permute-done | bytes 49184 | tf_op jit(solution)/shard_map/ppermute | solution.py:237
  33.0 4.4 %collective-permute-done.5 = bf16[96,256]{1,0:T(8,128)(2,1)S(1)} collective-permute-done((bf16[96,256]{1,0:T(8,128)(2,1)S(1)}, bf16[96,256]{1,0:T(8,128)(2,1)S(1)}, u32[]{:S(2)}, u32[]{:S(2)}) %collective-permute-start.5) | collective-permute-done | bytes 49184 | tf_op jit(solution)/shard_map/ppermute | solution.py:237
  37.4 1.3 %collective-permute-start.10 = (bf16[96,256]{1,0:T(8,128)(2,1)S(1)}, bf16[96,256]{1,0:T(8,128)(2,1)S(1)}, u32[]{:S(2)}, u32[]{:S(2)}) collective-permute-start(bf16[96,256]{1,0:T(8,128)(2,1)S(1)} %add_convert_fusion.refs_0_), channel_id=1, source_target_pairs={{0,48},{16,32},{32,16},{48,0},{1,49},{17,33},{33,17},{49,1},{2,50}... | collective-permute-start | bytes 147464 | tf_op jit(solution)/shard_map/ppermute | solution.py:237
  38.7 2.6 %collective-permute-start.8 = (bf16[96,256]{1,0:T(8,128)(2,1)S(1)}, bf16[96,256]{1,0:T(8,128)(2,1)S(1)}, u32[]{:S(2)}, u32[]{:S(2)}) collective-permute-start(bf16[96,256]{1,0:T(8,128)(2,1)S(1)} %add_convert_fusion.refs_0_), channel_id=1, source_target_pairs={{0,32},{16,48},{32,0},{48,16},{1,33},{17,49},{33,1},{49,17},{2,34}... | collective-permute-start | bytes 147464 | tf_op jit(solution)/shard_map/ppermute | solution.py:237
  41.4 0.3 collective-permute-done.10.refs_3_
  41.7 1.7 %collective-permute-done.8.refs_1_ = bf16[96,256]{1,0:T(8,128)(2,1)S(1)} collective-permute-done((bf16[96,256]{1,0:T(8,128)(2,1)S(1)}, bf16[96,256]{1,0:T(8,128)(2,1)S(1)}, u32[]{:S(2)}, u32[]{:S(2)}) %collective-permute-start.8) | collective-permute-done | bytes 49184 | tf_op jit(solution)/shard_map/ppermute | solution.py:237
  43.4 5.0 %collective-permute-start.11 = (bf16[96,1024]{1,0:T(8,128)(2,1)S(1)}, bf16[96,1024]{1,0:T(8,128)(2,1)S(1)}, u32[]{:S(2)}, u32[]{:S(2)}) collective-permute-start(bf16[96,1024]{1,0:T(8,128)(2,1)S(1)} %pad_maximum_fusion), channel_id=1, source_target_pairs={{0,8},{8,0},{1,9},{9,1},{2,10},{10,2},{3,11},{11,3},{4,12},{12,4},... | collective-permute-start | bytes 589832 | tf_op jit(solution)/shard_map/ppermute | solution.py:237
  48.4 1.1 %collective-permute-done.11.refs_4_ = bf16[96,1024]{1,0:T(8,128)(2,1)S(1)} collective-permute-done((bf16[96,1024]{1,0:T(8,128)(2,1)S(1)}, bf16[96,1024]{1,0:T(8,128)(2,1)S(1)}, u32[]{:S(2)}, u32[]{:S(2)}) %collective-permute-start.11) | collective-permute-done | bytes 196640 | tf_op jit(solution)/shard_map/ppermute | solution.py:237
  49.5 0.5 product.1
  50.0 9.8 %all_to_all.5.shares_ref = bf16[8,48,128]{2,1,0:T(8,128)(2,1)S(1)} all-to-all(bf16[8,48,128]{2,1,0:T(8,128)(2,1)S(1)} %product.1), channel_id=1, replica_groups=mesh['zh'=4,'x'=4,'core'=2,'y'=4,'zl'=2] {'y','zl'}, dimensions={0} | all-to-all | bytes 196608 | tf_op jit(solution)/shard_map/all_to_all | solution.py:265
  59.8 0.8 %finish.1 = f32[64,96]{1,0:T(8,128)} custom-call(bf16[8,48,128]{2,1,0:T(8,128)(2,1)S(1)} %all_to_all.5.shares_ref), custom_call_target="tpu_custom_call" | custom-call | tf_op jit(solution)/shard_map/finish/pallas_call | solution.py:225
  (13 shorter events, 0.1 us)
Async XLA Ops:
  0.0 6.8 %collective-permute-start.1 = (bf16[96,4096]{1,0:T(8,128)(2,1)}, bf16[96,4096]{1,0:T(8,128)(2,1)S(1)}, u32[]{:S(2)}, u32[]{:S(2)}) collective-permute-start(bf16[96,4096]{1,0:T(8,128)(2,1)} %sens_in.1), channel_id=1, source_target_pairs={{0,8},{8,0},{1,9},{9,1},{2,10},{10,2},{3,11},{11,3},{4,12},{12,4},... | collective-permute-start | bytes 2359304 | tf_op jit(solution)/shard_map/ppermute | solution.py:237
  3.2 3.6 %collective-permute-start = (f32[3,4096]{1,0:T(4,128)}, f32[3,4096]{1,0:T(4,128)S(1)}, u32[]{:S(2)}, u32[]{:S(2)}) collective-permute-start(f32[3,4096]{1,0:T(4,128)} %node_in.1), channel_id=1, source_target_pairs={{0,8},{8,0},{1,9},{9,1},{2,10},{10,2},{3,11},{11,3},{4,12},{12,4},... | collective-permute-start | bytes 147464 | tf_op jit(solution)/shard_map/ppermute | solution.py:237
  12.6 10.4 %collective-permute-start.3 = (f32[96,256]{1,0:T(8,128)S(1)}, f32[96,256]{1,0:T(8,128)S(1)}, u32[]{:S(2)}, u32[]{:S(2)}) collective-permute-start(f32[96,256]{1,0:T(8,128)S(1)} %pull.4), channel_id=1, source_target_pairs={{0,16},{16,0},{32,48},{48,32},{1,17},{17,1},{33,49},{49,33},{2,18}... | collective-permute-start | bytes 294920 | tf_op jit(solution)/shard_map/ppermute | solution.py:237
  16.3 6.7 %collective-permute-start.4 = (f32[96,256]{1,0:T(8,128)S(1)}, f32[96,256]{1,0:T(8,128)S(1)}, u32[]{:S(2)}, u32[]{:S(2)}) collective-permute-start(f32[96,256]{1,0:T(8,128)S(1)} %pull.5), channel_id=1, source_target_pairs={{0,48},{16,32},{32,16},{48,0},{1,49},{17,33},{33,17},{49,1},{2,50}... | collective-permute-start | bytes 294920 | tf_op jit(solution)/shard_map/ppermute | solution.py:237
  17.7 31.7 %copy-start = (bf16[2048,512]{1,0:T(8,128)(2,1)S(1)}, bf16[2048,512]{1,0:T(8,128)(2,1)}, u32[]{:S(2)}) copy-start(bf16[2048,512]{1,0:T(8,128)(2,1)} %refs_5_.1) | copy-start | bytes 6291460
  17.7 5.3 %collective-permute-start.2 = (f32[96,256]{1,0:T(8,128)S(1)}, f32[96,256]{1,0:T(8,128)S(1)}, u32[]{:S(2)}, u32[]{:S(2)}) collective-permute-start(f32[96,256]{1,0:T(8,128)S(1)} %get-tuple-element.16), channel_id=1, source_target_pairs={{0,32},{16,48},{32,0},{48,16},{1,33},{17,49},{33,1},{49,17},{2,34}... | collective-permute-start | bytes 294920 | tf_op jit(solution)/shard_map/ppermute | solution.py:237
  23.1 8.0 %collective-permute-start.7 = (bf16[96,256]{1,0:T(8,128)(2,1)S(1)}, bf16[96,256]{1,0:T(8,128)(2,1)S(1)}, u32[]{:S(2)}, u32[]{:S(2)}) collective-permute-start(bf16[96,256]{1,0:T(8,128)(2,1)S(1)} %get-tuple-element.17), channel_id=1, source_target_pairs={{0,192},{64,128},{128,64},{192,0},{1,193},{65,129},{129,65},{193,1... | collective-permute-start | bytes 147464 | tf_op jit(solution)/shard_map/ppermute | solution.py:237
  28.9 4.1 %collective-permute-start.6 = (bf16[96,256]{1,0:T(8,128)(2,1)S(1)}, bf16[96,256]{1,0:T(8,128)(2,1)S(1)}, u32[]{:S(2)}, u32[]{:S(2)}) collective-permute-start(bf16[96,256]{1,0:T(8,128)(2,1)S(1)} %get-tuple-element.17), channel_id=1, source_target_pairs={{0,64},{64,0},{128,192},{192,128},{1,65},{65,1},{129,193},{193,129... | collective-permute-start | bytes 147464 | tf_op jit(solution)/shard_map/ppermute | solution.py:237
  30.1 7.3 %collective-permute-start.5 = (bf16[96,256]{1,0:T(8,128)(2,1)S(1)}, bf16[96,256]{1,0:T(8,128)(2,1)S(1)}, u32[]{:S(2)}, u32[]{:S(2)}) collective-permute-start(bf16[96,256]{1,0:T(8,128)(2,1)S(1)} %get-tuple-element.17), channel_id=1, source_target_pairs={{0,128},{64,192},{128,0},{192,64},{1,129},{65,193},{129,1},{193,65... | collective-permute-start | bytes 147464 | tf_op jit(solution)/shard_map/ppermute | solution.py:237
  37.4 4.2 %collective-permute-start.10 = (bf16[96,256]{1,0:T(8,128)(2,1)S(1)}, bf16[96,256]{1,0:T(8,128)(2,1)S(1)}, u32[]{:S(2)}, u32[]{:S(2)}) collective-permute-start(bf16[96,256]{1,0:T(8,128)(2,1)S(1)} %add_convert_fusion.refs_0_), channel_id=1, source_target_pairs={{0,48},{16,32},{32,16},{48,0},{1,49},{17,33},{33,17},{49,1},{2,50}... | collective-permute-start | bytes 147464 | tf_op jit(solution)/shard_map/ppermute | solution.py:237
  38.7 2.9 %collective-permute-start.9 = (bf16[96,256]{1,0:T(8,128)(2,1)S(1)}, bf16[96,256]{1,0:T(8,128)(2,1)S(1)}, u32[]{:S(2)}, u32[]{:S(2)}) collective-permute-start(bf16[96,256]{1,0:T(8,128)(2,1)S(1)} %add_convert_fusion.refs_0_), channel_id=1, source_target_pairs={{0,16},{16,0},{32,48},{48,32},{1,17},{17,1},{33,49},{49,33},{2,18}... | collective-permute-start | bytes 147464 | tf_op jit(solution)/shard_map/ppermute | solution.py:237
  38.7 4.6 %collective-permute-start.8 = (bf16[96,256]{1,0:T(8,128)(2,1)S(1)}, bf16[96,256]{1,0:T(8,128)(2,1)S(1)}, u32[]{:S(2)}, u32[]{:S(2)}) collective-permute-start(bf16[96,256]{1,0:T(8,128)(2,1)S(1)} %add_convert_fusion.refs_0_), channel_id=1, source_target_pairs={{0,32},{16,48},{32,0},{48,16},{1,33},{17,49},{33,1},{49,17},{2,34}... | collective-permute-start | bytes 147464 | tf_op jit(solution)/shard_map/ppermute | solution.py:237
  43.4 6.1 %collective-permute-start.11 = (bf16[96,1024]{1,0:T(8,128)(2,1)S(1)}, bf16[96,1024]{1,0:T(8,128)(2,1)S(1)}, u32[]{:S(2)}, u32[]{:S(2)}) collective-permute-start(bf16[96,1024]{1,0:T(8,128)(2,1)S(1)} %pad_maximum_fusion), channel_id=1, source_target_pairs={{0,8},{8,0},{1,9},{9,1},{2,10},{10,2},{3,11},{11,3},{4,12},{12,4},... | collective-permute-start | bytes 589832 | tf_op jit(solution)/shard_map/ppermute | solution.py:237

commit v3 on v2

--- a/solution.py
+++ b/solution.py
@@ -82,12 +82,13 @@
         copy.start()
     node_ref[...] = jnp.zeros_like(node_ref)
     ctrl_ref[...] = jnp.zeros_like(ctrl_ref)
-    for copy in copies:
-        copy.wait()
+    copies[0].wait()
     write_features(node_xyz, node_rows, True)
     node_ref[:, 0:used] = node_rows[...].T.astype(jnp.bfloat16)
+    copies[1].wait()
     write_features(ctrl_xyz, ctrl_rows, False)
     ctrl_ref[0:used, :] = ctrl_rows[...].astype(jnp.bfloat16)
+    copies[2].wait()
     out_ref[...] = pulled_block(node_ref, ctrl_ref, sens_ref, block_of(step))
 
 
@@ -240,18 +241,17 @@
 def per_device(sensitivity, node_xyz, ctrl_xyz, inverse):
     other_sens = swapped(sensitivity, "core", 1)
     other_xyz = swapped(node_xyz, "core", 1)
-    far, node_feat, sens, ctrl_feat = first_pull(
-        2, sensitivity, node_xyz, ctrl_xyz
-    )
-    far, other_feat = second_pull(2, far, other_xyz, other_sens, ctrl_feat)
+    near, node_feat, sens, ctrl_feat = first_pull(1, sensitivity, node_xyz, ctrl_xyz)
+    near, other_feat = second_pull(1, near, other_xyz, other_sens, ctrl_feat)
     prepared = (node_feat, sens, other_feat, other_sens, ctrl_feat)
-    parts = [swapped(far, "x", 2)]
-    for step in (1, 3):
-        block = pull(step, *prepared)
-        parts.append(swapped(block, "x", step))
+
+    far = pull(2, *prepared)
+    two = jnp.concatenate([near, far], axis=1).astype(jnp.bfloat16)
+    two = swapped(two, "x", 1).astype(jnp.float32)
+    right = pull(3, *prepared)
+    right = swapped(right + two[:, span:], "x", 3)
     summed = pull(0, *prepared)
-    for part in parts:
-        summed = summed + part
+    summed = summed + two[:, :span] + right
 
     low = summed.astype(jnp.bfloat16)
     for by in (2, 1, 3):

time: 61.5 us -> 59.8 us (0.972)
  starting transfers between devices: 23.7 us -> 21.4 us
  waiting for transfers between devices: 9.37 us -> 10.2 us
    ppermute x12 -> x11, starting transfers between devices: 23.7 us -> 21.4 us  [swapped(): return lax.ppermute(value, axis, [(i, i ^ by) for i in range(size)])]
    ppermute x12 -> x11, waiting for transfers between devices: 9.37 us -> 10.2 us  [swapped(): return lax.ppermute(value, axis, [(i, i ^ by) for i in range(size)])]
  transfers between devices with their start and end apart: 12 -> 11, of which waited for: 5 -> 8; matrix products, arithmetic and copies ran while one was open for 0% -> 0% of each run, Pallas kernels for 17% -> 17%
where the time goes in v3:
time: 59.8 us; the launch traced here: 58.8 us
  starting transfers between devices  21.4 us (36%)
  Pallas kernels  17.2 us (29%)
  waiting for transfers between devices  10.2 us (17%)
  blocking collectives  9.77 us (16%)
    ppermute x11, starting transfers between devices, swapped(): return lax.ppermute(value, axis, [(i, i ^ by) for i in range(size)])  21.4 us
    pallas_call x3, Pallas kernels, pull(): pl.pallas_call(functools.partial(pull_kernel, step), out_shape=jax.ShapeD...  10.2 us
    ppermute x11, waiting for transfers between devices, swapped(): return lax.ppermute(value, axis, [(i, i ^ by) for i in range(size)])  10.2 us
    all_to_all x1, blocking collectives, per_device(): lax.all_to_all(shares, ('y', 'zl'), split_axis=0, concat_axis=0, tiled=True)  9.77 us
    pallas_call x1, Pallas kernels, first_pull(): pl.pallas_call(functools.partial(first_kernel, step), out_shape=[jax.Shap...  3.31 us
    pallas_call x1, Pallas kernels, second_pull(): pl.pallas_call(functools.partial(second_kernel, step), out_shape=[jax.Sha...  2.39 us
  transfers between devices with their start and end apart: 11, of which 8 were waited for; matrix products, arithmetic and copies ran while one was open for 0% of the time, Pallas kernels for 17%

profile of v3, /device:TPU:1, one launch (start us, length us, event | category | flops | bytes accessed | tf_op | source)
XLA Modules:
  0.0 58.8 jit_solution(12756757863960619501)
XLA Ops:
  0.0 3.2 %collective-permute-start.1 = (bf16[96,4096]{1,0:T(8,128)(2,1)}, bf16[96,4096]{1,0:T(8,128)(2,1)S(1)}, u32[]{:S(2)}, u32[]{:S(2)}) collective-permute-start(bf16[96,4096]{1,0:T(8,128)(2,1)} %sens_in.1), channel_id=1, source_target_pairs={{0,8},{8,0},{1,9},{9,1},{2,10},{10,2},{3,11},{11,3},{4,12},{12,4},... | collective-permute-start | bytes 2359304 | tf_op jit(solution)/shard_map/ppermute | solution.py:238
  3.2 3.3 %first_pull.1 = (f32[96,256]{1,0:T(8,128)S(1)}, bf16[4096,128]{1,0:T(8,128)(2,1)S(1)}, bf16[96,4096]{1,0:T(8,128)(2,1)S(1)}, bf16[128,2048]{1,0:T(8,128)(2,1)S(1)}) custom-call(bf16[96,4096]{1,0:T(8,128)(2,1)} %sens_in.1, f32[3,4096]{1,0:T(4,128)} %node_in.1, f32[3,2048]{1,0:T(4,128)} %ctrl_in.1), custom_call_target="tpu_custom_call" | custom-call | flops 419430400 | bytes 1835008 | tf_op jit(solution)/shard_map/first_pull/pallas_call | solution.py:106
  6.5 2.4 %second_pull.1 = (f32[96,256]{1,0:T(8,128)S(1)}, bf16[4096,128]{1,0:T(8,128)(2,1)S(1)}) custom-call(f32[96,256]{1,0:T(8,128)S(1)} %get-tuple-element.13.part_ref, f32[3,4096]{1,0:T(4,128)S(1)} %collective-permute-done.node_xyz, bf16[96,4096]{1,0:T(8,128)(2,1)S(1)} %collective-permute-done.1.sens_ref.sens_b, bf16[128,2048]{1,0:T(8,128)(2,1)S(1)} %get-tuple-element.14.ctrl_ref), custom_call_target="tpu_custom_call" | custom-call | flops 419430400 | bytes 1835008 | tf_op jit(solution)/shard_map/second_pull/pallas_call | solution.py:141
  9.0 3.4 %pull.4 = f32[96,256]{1,0:T(8,128)S(1)} custom-call(bf16[4096,128]{1,0:T(8,128)(2,1)S(1)} %get-tuple-element.11.node_a, bf16[96,4096]{1,0:T(8,128)(2,1)S(1)} %get-tuple-element.12.sens_a, bf16[4096,128]{1,0:T(8,128)(2,1)S(1)} %get-tuple-element.15.node_b, bf16[96,4096]{1,0:T(8,128)(2,1)S(1)} %collective-permute-done.1.sens_ref.sens_b, ...), custom_call_target="tpu_custom_call" | custom-call | flops 838860800 | bytes 1835008 | tf_op jit(solution)/shard_map/pull/pallas_call | solution.py:164
  12.4 0.3 collective-permute-start.2
  12.7 3.4 %pull.5 = f32[96,256]{1,0:T(8,128)S(1)} custom-call(bf16[4096,128]{1,0:T(8,128)(2,1)S(1)} %get-tuple-element.11.node_a, bf16[96,4096]{1,0:T(8,128)(2,1)S(1)} %get-tuple-element.12.sens_a, bf16[4096,128]{1,0:T(8,128)(2,1)S(1)} %get-tuple-element.15.node_b, bf16[96,4096]{1,0:T(8,128)(2,1)S(1)} %collective-permute-done.1.sens_ref.sens_b, ...), custom_call_target="tpu_custom_call" | custom-call | flops 838860800 | bytes 1835008 | tf_op jit(solution)/shard_map/pull/pallas_call | solution.py:164
  16.1 0.4 collective-permute-done.2
  16.6 1.0 %collective-permute-start.3 = (f32[96,256]{1,0:T(8,128)S(1)}, f32[96,256]{1,0:T(8,128)S(1)}, u32[]{:S(2)}, u32[]{:S(2)}) collective-permute-start(f32[96,256]{1,0:T(8,128)S(1)} %slice_add_fusion), channel_id=1, source_target_pairs={{0,48},{16,32},{32,16},{48,0},{1,49},{17,33},{33,17},{49,1},{2,50}... | collective-permute-start | bytes 294920 | tf_op jit(solution)/shard_map/ppermute | solution.py:238
  17.5 3.4 %pull.3 = f32[96,256]{1,0:T(8,128)S(1)} custom-call(bf16[4096,128]{1,0:T(8,128)(2,1)S(1)} %get-tuple-element.11.node_a, bf16[96,4096]{1,0:T(8,128)(2,1)S(1)} %get-tuple-element.12.sens_a, bf16[4096,128]{1,0:T(8,128)(2,1)S(1)} %get-tuple-element.15.node_b, bf16[96,4096]{1,0:T(8,128)(2,1)S(1)} %collective-permute-done.1.sens_ref.sens_b, ...), custom_call_target="tpu_custom_call" | custom-call | flops 838860800 | bytes 1835008 | tf_op jit(solution)/shard_map/pull/pallas_call | solution.py:164
  20.9 0.4 collective-permute-done.3
  21.4 5.7 %collective-permute-start.6 = (bf16[96,256]{1,0:T(8,128)(2,1)S(1)}, bf16[96,256]{1,0:T(8,128)(2,1)S(1)}, u32[]{:S(2)}, u32[]{:S(2)}) collective-permute-start(bf16[96,256]{1,0:T(8,128)(2,1)S(1)} %fusion.1), channel_id=1, source_target_pairs={{0,192},{64,128},{128,64},{192,0},{1,193},{65,129},{129,65},{193,1... | collective-permute-start | bytes 147464 | tf_op jit(solution)/shard_map/ppermute | solution.py:238
  27.1 1.2 %collective-permute-start.5 = (bf16[96,256]{1,0:T(8,128)(2,1)S(1)}, bf16[96,256]{1,0:T(8,128)(2,1)S(1)}, u32[]{:S(2)}, u32[]{:S(2)}) collective-permute-start(bf16[96,256]{1,0:T(8,128)(2,1)S(1)} %fusion.1), channel_id=1, source_target_pairs={{0,64},{64,0},{128,192},{192,128},{1,65},{65,1},{129,193},{193,129... | collective-permute-start | bytes 147464 | tf_op jit(solution)/shard_map/ppermute | solution.py:238
  28.2 1.0 %collective-permute-start.4 = (bf16[96,256]{1,0:T(8,128)(2,1)S(1)}, bf16[96,256]{1,0:T(8,128)(2,1)S(1)}, u32[]{:S(2)}, u32[]{:S(2)}) collective-permute-start(bf16[96,256]{1,0:T(8,128)(2,1)S(1)} %fusion.1), channel_id=1, source_target_pairs={{0,128},{64,192},{128,0},{192,64},{1,129},{65,193},{129,1},{193,65... | collective-permute-start | bytes 147464 | tf_op jit(solution)/shard_map/ppermute | solution.py:238
  29.3 1.8 %collective-permute-done.5 = bf16[96,256]{1,0:T(8,128)(2,1)S(1)} collective-permute-done((bf16[96,256]{1,0:T(8,128)(2,1)S(1)}, bf16[96,256]{1,0:T(8,128)(2,1)S(1)}, u32[]{:S(2)}, u32[]{:S(2)}) %collective-permute-start.5) | collective-permute-done | bytes 49184 | tf_op jit(solution)/shard_map/ppermute | solution.py:238
  31.1 4.4 %collective-permute-done.4 = bf16[96,256]{1,0:T(8,128)(2,1)S(1)} collective-permute-done((bf16[96,256]{1,0:T(8,128)(2,1)S(1)}, bf16[96,256]{1,0:T(8,128)(2,1)S(1)}, u32[]{:S(2)}, u32[]{:S(2)}) %collective-permute-start.4) | collective-permute-done | bytes 49184 | tf_op jit(solution)/shard_map/ppermute | solution.py:238
  35.5 1.4 %collective-permute-start.9 = (bf16[96,256]{1,0:T(8,128)(2,1)S(1)}, bf16[96,256]{1,0:T(8,128)(2,1)S(1)}, u32[]{:S(2)}, u32[]{:S(2)}) collective-permute-start(bf16[96,256]{1,0:T(8,128)(2,1)S(1)} %add_convert_fusion.refs_0_), channel_id=1, source_target_pairs={{0,48},{16,32},{32,16},{48,0},{1,49},{17,33},{33,17},{49,1},{2,50}... | collective-permute-start | bytes 147464 | tf_op jit(solution)/shard_map/ppermute | solution.py:238
  37.0 2.5 %collective-permute-start.7 = (bf16[96,256]{1,0:T(8,128)(2,1)S(1)}, bf16[96,256]{1,0:T(8,128)(2,1)S(1)}, u32[]{:S(2)}, u32[]{:S(2)}) collective-permute-start(bf16[96,256]{1,0:T(8,128)(2,1)S(1)} %add_convert_fusion.refs_0_), channel_id=1, source_target_pairs={{0,32},{16,48},{32,0},{48,16},{1,33},{17,49},{33,1},{49,17},{2,34}... | collective-permute-start | bytes 147464 | tf_op jit(solution)/shard_map/ppermute | solution.py:238
  39.5 0.3 collective-permute-done.9.refs_3_
  39.9 1.6 %collective-permute-done.7.refs_1_ = bf16[96,256]{1,0:T(8,128)(2,1)S(1)} collective-permute-done((bf16[96,256]{1,0:T(8,128)(2,1)S(1)}, bf16[96,256]{1,0:T(8,128)(2,1)S(1)}, u32[]{:S(2)}, u32[]{:S(2)}) %collective-permute-start.7) | collective-permute-done | bytes 49184 | tf_op jit(solution)/shard_map/ppermute | solution.py:238
  41.5 5.1 %collective-permute-start.10 = (bf16[96,1024]{1,0:T(8,128)(2,1)S(1)}, bf16[96,1024]{1,0:T(8,128)(2,1)S(1)}, u32[]{:S(2)}, u32[]{:S(2)}) collective-permute-start(bf16[96,1024]{1,0:T(8,128)(2,1)S(1)} %pad_maximum_fusion), channel_id=1, source_target_pairs={{0,8},{8,0},{1,9},{9,1},{2,10},{10,2},{3,11},{11,3},{4,12},{12,4},... | collective-permute-start | bytes 589832 | tf_op jit(solution)/shard_map/ppermute | solution.py:238
  46.7 1.1 %collective-permute-done.10.refs_4_ = bf16[96,1024]{1,0:T(8,128)(2,1)S(1)} collective-permute-done((bf16[96,1024]{1,0:T(8,128)(2,1)S(1)}, bf16[96,1024]{1,0:T(8,128)(2,1)S(1)}, u32[]{:S(2)}, u32[]{:S(2)}) %collective-permute-start.10) | collective-permute-done | bytes 196640 | tf_op jit(solution)/shard_map/ppermute | solution.py:238
  47.7 0.5 product.1
  48.3 9.8 %all_to_all.5.shares_ref = bf16[8,48,128]{2,1,0:T(8,128)(2,1)S(1)} all-to-all(bf16[8,48,128]{2,1,0:T(8,128)(2,1)S(1)} %product.1), channel_id=1, replica_groups=mesh['zh'=4,'x'=4,'core'=2,'y'=4,'zl'=2] {'y','zl'}, dimensions={0} | all-to-all | bytes 196608 | tf_op jit(solution)/shard_map/all_to_all | solution.py:265
  58.1 0.8 %finish.1 = f32[64,96]{1,0:T(8,128)} custom-call(bf16[8,48,128]{2,1,0:T(8,128)(2,1)S(1)} %all_to_all.5.shares_ref), custom_call_target="tpu_custom_call" | custom-call | tf_op jit(solution)/shard_map/finish/pallas_call | solution.py:226
  (16 shorter events, 0.3 us)
Async XLA Ops:
  0.0 6.5 %collective-permute-start.1 = (bf16[96,4096]{1,0:T(8,128)(2,1)}, bf16[96,4096]{1,0:T(8,128)(2,1)S(1)}, u32[]{:S(2)}, u32[]{:S(2)}) collective-permute-start(bf16[96,4096]{1,0:T(8,128)(2,1)} %sens_in.1), channel_id=1, source_target_pairs={{0,8},{8,0},{1,9},{9,1},{2,10},{10,2},{3,11},{11,3},{4,12},{12,4},... | collective-permute-start | bytes 2359304 | tf_op jit(solution)/shard_map/ppermute | solution.py:238
  3.2 3.3 %collective-permute-start = (f32[3,4096]{1,0:T(4,128)}, f32[3,4096]{1,0:T(4,128)S(1)}, u32[]{:S(2)}, u32[]{:S(2)}) collective-permute-start(f32[3,4096]{1,0:T(4,128)} %node_in.1), channel_id=1, source_target_pairs={{0,8},{8,0},{1,9},{9,1},{2,10},{10,2},{3,11},{11,3},{4,12},{12,4},... | collective-permute-start | bytes 147464 | tf_op jit(solution)/shard_map/ppermute | solution.py:238
  12.4 4.1 %collective-permute-start.2 = (bf16[96,512]{1,0:T(8,128)(2,1)S(1)}, bf16[96,512]{1,0:T(8,128)(2,1)S(1)}, u32[]{:S(2)}, u32[]{:S(2)}) collective-permute-start(bf16[96,512]{1,0:T(8,128)(2,1)S(1)} %pad_maximum_fusion.1), channel_id=1, source_target_pairs={{0,16},{16,0},{32,48},{48,32},{1,17},{17,1},{33,49},{49,33},{2,18}... | collective-permute-start | bytes 294920 | tf_op jit(solution)/shard_map/ppermute | solution.py:238
  16.6 31.2 %copy-start = (bf16[2048,512]{1,0:T(8,128)(2,1)S(1)}, bf16[2048,512]{1,0:T(8,128)(2,1)}, u32[]{:S(2)}) copy-start(bf16[2048,512]{1,0:T(8,128)(2,1)} %refs_5_.1) | copy-start | bytes 6291460
  16.6 4.8 %collective-permute-start.3 = (f32[96,256]{1,0:T(8,128)S(1)}, f32[96,256]{1,0:T(8,128)S(1)}, u32[]{:S(2)}, u32[]{:S(2)}) collective-permute-start(f32[96,256]{1,0:T(8,128)S(1)} %slice_add_fusion), channel_id=1, source_target_pairs={{0,48},{16,32},{32,16},{48,0},{1,49},{17,33},{33,17},{49,1},{2,50}... | collective-permute-start | bytes 294920 | tf_op jit(solution)/shard_map/ppermute | solution.py:238
  21.4 7.9 %collective-permute-start.6 = (bf16[96,256]{1,0:T(8,128)(2,1)S(1)}, bf16[96,256]{1,0:T(8,128)(2,1)S(1)}, u32[]{:S(2)}, u32[]{:S(2)}) collective-permute-start(bf16[96,256]{1,0:T(8,128)(2,1)S(1)} %fusion.1), channel_id=1, source_target_pairs={{0,192},{64,128},{128,64},{192,0},{1,193},{65,129},{129,65},{193,1... | collective-permute-start | bytes 147464 | tf_op jit(solution)/shard_map/ppermute | solution.py:238
  27.1 4.0 %collective-permute-start.5 = (bf16[96,256]{1,0:T(8,128)(2,1)S(1)}, bf16[96,256]{1,0:T(8,128)(2,1)S(1)}, u32[]{:S(2)}, u32[]{:S(2)}) collective-permute-start(bf16[96,256]{1,0:T(8,128)(2,1)S(1)} %fusion.1), channel_id=1, source_target_pairs={{0,64},{64,0},{128,192},{192,128},{1,65},{65,1},{129,193},{193,129... | collective-permute-start | bytes 147464 | tf_op jit(solution)/shard_map/ppermute | solution.py:238
  28.2 7.3 %collective-permute-start.4 = (bf16[96,256]{1,0:T(8,128)(2,1)S(1)}, bf16[96,256]{1,0:T(8,128)(2,1)S(1)}, u32[]{:S(2)}, u32[]{:S(2)}) collective-permute-start(bf16[96,256]{1,0:T(8,128)(2,1)S(1)} %fusion.1), channel_id=1, source_target_pairs={{0,128},{64,192},{128,0},{192,64},{1,129},{65,193},{129,1},{193,65... | collective-permute-start | bytes 147464 | tf_op jit(solution)/shard_map/ppermute | solution.py:238
  35.5 4.2 %collective-permute-start.9 = (bf16[96,256]{1,0:T(8,128)(2,1)S(1)}, bf16[96,256]{1,0:T(8,128)(2,1)S(1)}, u32[]{:S(2)}, u32[]{:S(2)}) collective-permute-start(bf16[96,256]{1,0:T(8,128)(2,1)S(1)} %add_convert_fusion.refs_0_), channel_id=1, source_target_pairs={{0,48},{16,32},{32,16},{48,0},{1,49},{17,33},{33,17},{49,1},{2,50}... | collective-permute-start | bytes 147464 | tf_op jit(solution)/shard_map/ppermute | solution.py:238
  37.0 2.9 %collective-permute-start.8 = (bf16[96,256]{1,0:T(8,128)(2,1)S(1)}, bf16[96,256]{1,0:T(8,128)(2,1)S(1)}, u32[]{:S(2)}, u32[]{:S(2)}) collective-permute-start(bf16[96,256]{1,0:T(8,128)(2,1)S(1)} %add_convert_fusion.refs_0_), channel_id=1, source_target_pairs={{0,16},{16,0},{32,48},{48,32},{1,17},{17,1},{33,49},{49,33},{2,18}... | collective-permute-start | bytes 147464 | tf_op jit(solution)/shard_map/ppermute | solution.py:238
  37.0 4.5 %collective-permute-start.7 = (bf16[96,256]{1,0:T(8,128)(2,1)S(1)}, bf16[96,256]{1,0:T(8,128)(2,1)S(1)}, u32[]{:S(2)}, u32[]{:S(2)}) collective-permute-start(bf16[96,256]{1,0:T(8,128)(2,1)S(1)} %add_convert_fusion.refs_0_), channel_id=1, source_target_pairs={{0,32},{16,48},{32,0},{48,16},{1,33},{17,49},{33,1},{49,17},{2,34}... | collective-permute-start | bytes 147464 | tf_op jit(solution)/shard_map/ppermute | solution.py:238
  41.5 6.2 %collective-permute-start.10 = (bf16[96,1024]{1,0:T(8,128)(2,1)S(1)}, bf16[96,1024]{1,0:T(8,128)(2,1)S(1)}, u32[]{:S(2)}, u32[]{:S(2)}) collective-permute-start(bf16[96,1024]{1,0:T(8,128)(2,1)S(1)} %pad_maximum_fusion), channel_id=1, source_target_pairs={{0,8},{8,0},{1,9},{9,1},{2,10},{10,2},{3,11},{11,3},{4,12},{12,4},... | collective-permute-start | bytes 589832 | tf_op jit(solution)/shard_map/ppermute | solution.py:238

commit v4 on v3

--- a/solution.py
+++ b/solution.py
@@ -14,7 +14,7 @@
 used = 40
 span = 256
 whole = pl.BlockSpec(memory_space=pltpu.VMEM)
-params = pltpu.CompilerParams(vmem_limit_bytes=16 * 1024 * 1024)
+params = pltpu.CompilerParams(vmem_limit_bytes=20 * 1024 * 1024)
 
 
 def pieces_of(values):
@@ -46,21 +46,51 @@
 
 
 def wendland(squared):
-    squared = jnp.maximum(squared, 1e-30)
     r4 = squared * lax.rsqrt(squared)
     remain = jnp.maximum(4.0 - r4, 0.0)
     remain2 = remain * remain
     return (remain2 * remain2 * (r4 + 1.0)).astype(jnp.bfloat16)
 
 
-def pulled_block(node_ref, ctrl_ref, sens_ref, block):
+tile = 512
+
+
+def block_scratch(nodes):
+    return [
+        pltpu.VMEM((nodes, span), jnp.float32),
+        pltpu.VMEM((nodes, span), jnp.bfloat16),
+    ]
+
+
+def pulled_block(node_ref, ctrl_ref, sens_ref, block, squares, weights):
     columns = pl.ds(pl.multiple_of(block * span, span), span)
-    squared = jnp.dot(
-        node_ref[...], ctrl_ref[:, columns], preferred_element_type=jnp.float32
-    )
-    total = jnp.dot(
-        sens_ref[...], wendland(squared), preferred_element_type=jnp.float32
-    )
+    tiles = node_ref.shape[0] // tile
+
+    def square(i):
+        at = slice(i * tile, (i + 1) * tile)
+        product = jnp.dot(
+            node_ref[at, :], ctrl_ref[:, columns], preferred_element_type=jnp.float32
+        )
+        squares[at, :] = jnp.maximum(product, 1e-30)
+
+    def gather(i):
+        at = slice(i * tile, (i + 1) * tile)
+        return jnp.dot(
+            sens_ref[:, at], weights[at, :], preferred_element_type=jnp.float32
+        )
+
+    total = None
+    square(0)
+    for i in range(tiles):
+        if i + 1 < tiles:
+            square(i + 1)
+        at = slice(i * tile, (i + 1) * tile)
+        weights[at, :] = wendland(squares[at, :])
+        if i > 0:
+            term = gather(i - 1)
+            total = term if total is None else total + term
+    last = gather(tiles - 1)
+    total = last if total is None else total + last
     return total * (1.0 / 256.0)
 
 
@@ -71,7 +101,7 @@
 def first_kernel(
     step, sens_in, node_in, ctrl_in, out_ref, node_ref, sens_ref, ctrl_ref, *scratch
 ):
-    node_xyz, ctrl_xyz, node_rows, ctrl_rows, done = scratch
+    node_xyz, ctrl_xyz, node_rows, ctrl_rows, done, squares, weights = scratch
     copies = [
         pltpu.make_async_copy(source, target, done.at[i])
         for i, (source, target) in enumerate(
@@ -89,7 +119,9 @@
     write_features(ctrl_xyz, ctrl_rows, False)
     ctrl_ref[0:used, :] = ctrl_rows[...].astype(jnp.bfloat16)
     copies[2].wait()
-    out_ref[...] = pulled_block(node_ref, ctrl_ref, sens_ref, block_of(step))
+    out_ref[...] = pulled_block(
+        node_ref, ctrl_ref, sens_ref, block_of(step), squares, weights
+    )
 
 
 def pull_cost(nodes, blocks):
@@ -119,7 +151,8 @@
             pltpu.VMEM((used, nodes), jnp.float32),
             pltpu.VMEM((used, ctrls), jnp.float32),
             pltpu.SemaphoreType.DMA((3,)),
-        ],
+        ]
+        + block_scratch(nodes),
         cost_estimate=pull_cost(nodes, 1),
         compiler_params=params,
         name="first_pull",
@@ -127,12 +160,12 @@
 
 
 def second_kernel(
-    step, part_ref, node_xyz, sens_ref, ctrl_ref, out_ref, node_ref, node_rows
+    step, part_ref, node_xyz, sens_ref, ctrl_ref, out_ref, node_ref, node_rows, *scratch
 ):
     node_ref[...] = jnp.zeros_like(node_ref)
     write_features(node_xyz, node_rows, True)
     node_ref[:, 0:used] = node_rows[...].T.astype(jnp.bfloat16)
-    total = pulled_block(node_ref, ctrl_ref, sens_ref, block_of(step))
+    total = pulled_block(node_ref, ctrl_ref, sens_ref, block_of(step), *scratch)
     out_ref[...] = total + part_ref[...]
 
 
@@ -146,17 +179,17 @@
         ],
         in_specs=[whole] * 4,
         out_specs=[whole] * 2,
-        scratch_shapes=[pltpu.VMEM((used, nodes), jnp.float32)],
+        scratch_shapes=[pltpu.VMEM((used, nodes), jnp.float32)] + block_scratch(nodes),
         cost_estimate=pull_cost(nodes, 1),
         compiler_params=params,
         name="second_pull",
     )(part, node_xyz, sens, ctrl_feat)
 
 
-def pull_kernel(step, node_a, sens_a, node_b, sens_b, ctrl_ref, out_ref):
+def pull_kernel(step, node_a, sens_a, node_b, sens_b, ctrl_ref, out_ref, *scratch):
     block = block_of(step)
-    total = pulled_block(node_a, ctrl_ref, sens_a, block)
-    out_ref[...] = total + pulled_block(node_b, ctrl_ref, sens_b, block)
+    total = pulled_block(node_a, ctrl_ref, sens_a, block, *scratch[:2])
+    out_ref[...] = total + pulled_block(node_b, ctrl_ref, sens_b, block, *scratch[2:])
 
 
 def pull(step, *prepared):
@@ -166,6 +199,7 @@
         out_shape=jax.ShapeDtypeStruct((rows, span), jnp.float32),
         in_specs=[whole] * len(prepared),
         out_specs=whole,
+        scratch_shapes=block_scratch(nodes) * 2,
         cost_estimate=pull_cost(nodes, 2),
         compiler_params=params,
         name="pull",
@@ -249,7 +283,8 @@
     two = jnp.concatenate([near, far], axis=1).astype(jnp.bfloat16)
     two = swapped(two, "x", 1).astype(jnp.float32)
     right = pull(3, *prepared)
-    right = swapped(right + two[:, span:], "x", 3)
+    right = (right + two[:, span:]).astype(jnp.bfloat16)
+    right = swapped(right, "x", 3).astype(jnp.float32)
     summed = pull(0, *prepared)
     summed = summed + two[:, :span] + right
 

time: 59.8 us -> 59.3 us (level)
  transfers between devices with their start and end apart: 11 -> 11, of which waited for: 8 -> 6; matrix products, arithmetic and copies ran while one was open for 0% -> 0% of each run, Pallas kernels for 17% -> 17%
where the time goes in v4:
time: 59.3 us; the launch traced here: 58.4 us
  starting transfers between devices  21.3 us (36%)
  Pallas kernels  17.3 us (29%)
  blocking collectives  9.77 us (16%)
  waiting for transfers between devices  9.75 us (16%)
    ppermute x11, starting transfers between devices, swapped(): return lax.ppermute(value, axis, [(i, i ^ by) for i in range(size)])  21.3 us
    pallas_call x3, Pallas kernels, pull(): pl.pallas_call(functools.partial(pull_kernel, step), out_shape=jax.ShapeD...  10.1 us
    all_to_all x1, blocking collectives, per_device(): lax.all_to_all(shares, ('y', 'zl'), split_axis=0, concat_axis=0, tiled=True)  9.77 us
    ppermute x11, waiting for transfers between devices, swapped(): return lax.ppermute(value, axis, [(i, i ^ by) for i in range(size)])  9.75 us
    pallas_call x1, Pallas kernels, first_pull(): pl.pallas_call(functools.partial(first_kernel, step), out_shape=[jax.Shap...  3.32 us
    pallas_call x1, Pallas kernels, second_pull(): pl.pallas_call(functools.partial(second_kernel, step), out_shape=[jax.Sha...  2.47 us
  transfers between devices with their start and end apart: 11, of which 6 were waited for; matrix products, arithmetic and copies ran while one was open for 0% of the time, Pallas kernels for 17%

profile of v4, /device:TPU:1, one launch (start us, length us, event | category | flops | bytes accessed | tf_op | source)
XLA Modules:
  0.0 58.4 jit_solution(7471820343886917047)
XLA Ops:
  0.0 3.2 %collective-permute-start.1 = (bf16[96,4096]{1,0:T(8,128)(2,1)}, bf16[96,4096]{1,0:T(8,128)(2,1)S(1)}, u32[]{:S(2)}, u32[]{:S(2)}) collective-permute-start(bf16[96,4096]{1,0:T(8,128)(2,1)} %sens_in.1), channel_id=1, source_target_pairs={{0,8},{8,0},{1,9},{9,1},{2,10},{10,2},{3,11},{11,3},{4,12},{12,4},... | collective-permute-start | bytes 2359304 | tf_op jit(solution)/shard_map/ppermute | solution.py:272
  3.2 3.3 %first_pull.1 = (f32[96,256]{1,0:T(8,128)S(1)}, bf16[4096,128]{1,0:T(8,128)(2,1)S(1)}, bf16[96,4096]{1,0:T(8,128)(2,1)S(1)}, bf16[128,2048]{1,0:T(8,128)(2,1)S(1)}) custom-call(bf16[96,4096]{1,0:T(8,128)(2,1)} %sens_in.1, f32[3,4096]{1,0:T(4,128)} %node_in.1, f32[3,2048]{1,0:T(4,128)} %ctrl_in.1), custom_call_target="tpu_custom_call" | custom-call | flops 419430400 | bytes 1835008 | tf_op jit(solution)/shard_map/first_pull/pallas_call | solution.py:138
  6.5 2.5 %second_pull.1 = (f32[96,256]{1,0:T(8,128)S(1)}, bf16[4096,128]{1,0:T(8,128)(2,1)S(1)}) custom-call(f32[96,256]{1,0:T(8,128)S(1)} %get-tuple-element.13.part_ref, f32[3,4096]{1,0:T(4,128)S(1)} %collective-permute-done.node_xyz, bf16[96,4096]{1,0:T(8,128)(2,1)S(1)} %collective-permute-done.1.sens_ref.sens_b, bf16[128,2048]{1,0:T(8,128)(2,1)S(1)} %get-tuple-element.14.ctrl_ref), custom_call_target="tpu_custom_call" | custom-call | flops 419430400 | bytes 1835008 | tf_op jit(solution)/shard_map/second_pull/pallas_call | solution.py:174
  9.0 3.4 %pull.4 = f32[96,256]{1,0:T(8,128)S(1)} custom-call(bf16[4096,128]{1,0:T(8,128)(2,1)S(1)} %get-tuple-element.11.node_a, bf16[96,4096]{1,0:T(8,128)(2,1)S(1)} %get-tuple-element.12.sens_a, bf16[4096,128]{1,0:T(8,128)(2,1)S(1)} %get-tuple-element.15.node_b, bf16[96,4096]{1,0:T(8,128)(2,1)S(1)} %collective-permute-done.1.sens_ref.sens_b, ...), custom_call_target="tpu_custom_call" | custom-call | flops 838860800 | bytes 1835008 | tf_op jit(solution)/shard_map/pull/pallas_call | solution.py:197
  12.5 0.3 collective-permute-start.2
  12.7 3.4 %pull.5 = f32[96,256]{1,0:T(8,128)S(1)} custom-call(bf16[4096,128]{1,0:T(8,128)(2,1)S(1)} %get-tuple-element.11.node_a, bf16[96,4096]{1,0:T(8,128)(2,1)S(1)} %get-tuple-element.12.sens_a, bf16[4096,128]{1,0:T(8,128)(2,1)S(1)} %get-tuple-element.15.node_b, bf16[96,4096]{1,0:T(8,128)(2,1)S(1)} %collective-permute-done.1.sens_ref.sens_b, ...), custom_call_target="tpu_custom_call" | custom-call | flops 838860800 | bytes 1835008 | tf_op jit(solution)/shard_map/pull/pallas_call | solution.py:197
  16.1 0.4 collective-permute-done.2
  16.6 0.0 copy-start
  16.6 0.9 %collective-permute-start.3 = (bf16[96,256]{1,0:T(8,128)(2,1)S(1)}, bf16[96,256]{1,0:T(8,128)(2,1)S(1)}, u32[]{:S(2)}, u32[]{:S(2)}) collective-permute-start(bf16[96,256]{1,0:T(8,128)(2,1)S(1)} %fusion), channel_id=1, source_target_pairs={{0,48},{16,32},{32,16},{48,0},{1,49},{17,33},{33,17},{49,1},{2,50}... | collective-permute-start | bytes 147464 | tf_op jit(solution)/shard_map/ppermute | solution.py:272
  17.6 3.4 %pull.3 = f32[96,256]{1,0:T(8,128)S(1)} custom-call(bf16[4096,128]{1,0:T(8,128)(2,1)S(1)} %get-tuple-element.11.node_a, bf16[96,4096]{1,0:T(8,128)(2,1)S(1)} %get-tuple-element.12.sens_a, bf16[4096,128]{1,0:T(8,128)(2,1)S(1)} %get-tuple-element.15.node_b, bf16[96,4096]{1,0:T(8,128)(2,1)S(1)} %collective-permute-done.1.sens_ref.sens_b, ...), custom_call_target="tpu_custom_call" | custom-call | flops 838860800 | bytes 1835008 | tf_op jit(solution)/shard_map/pull/pallas_call | solution.py:197
  21.0 6.1 %collective-permute-start.6 = (bf16[96,256]{1,0:T(8,128)(2,1)S(1)}, bf16[96,256]{1,0:T(8,128)(2,1)S(1)}, u32[]{:S(2)}, u32[]{:S(2)}) collective-permute-start(bf16[96,256]{1,0:T(8,128)(2,1)S(1)} %fusion.2), channel_id=1, source_target_pairs={{0,192},{64,128},{128,64},{192,0},{1,193},{65,129},{129,65},{193,1... | collective-permute-start | bytes 147464 | tf_op jit(solution)/shard_map/ppermute | solution.py:272
  27.1 1.2 %collective-permute-start.5 = (bf16[96,256]{1,0:T(8,128)(2,1)S(1)}, bf16[96,256]{1,0:T(8,128)(2,1)S(1)}, u32[]{:S(2)}, u32[]{:S(2)}) collective-permute-start(bf16[96,256]{1,0:T(8,128)(2,1)S(1)} %fusion.2), channel_id=1, source_target_pairs={{0,64},{64,0},{128,192},{192,128},{1,65},{65,1},{129,193},{193,129... | collective-permute-start | bytes 147464 | tf_op jit(solution)/shard_map/ppermute | solution.py:272
  28.3 1.0 %collective-permute-start.4 = (bf16[96,256]{1,0:T(8,128)(2,1)S(1)}, bf16[96,256]{1,0:T(8,128)(2,1)S(1)}, u32[]{:S(2)}, u32[]{:S(2)}) collective-permute-start(bf16[96,256]{1,0:T(8,128)(2,1)S(1)} %fusion.2), channel_id=1, source_target_pairs={{0,128},{64,192},{128,0},{192,64},{1,129},{65,193},{129,1},{193,65... | collective-permute-start | bytes 147464 | tf_op jit(solution)/shard_map/ppermute | solution.py:272
  29.3 1.8 %collective-permute-done.5 = bf16[96,256]{1,0:T(8,128)(2,1)S(1)} collective-permute-done((bf16[96,256]{1,0:T(8,128)(2,1)S(1)}, bf16[96,256]{1,0:T(8,128)(2,1)S(1)}, u32[]{:S(2)}, u32[]{:S(2)}) %collective-permute-start.5) | collective-permute-done | bytes 49184 | tf_op jit(solution)/shard_map/ppermute | solution.py:272
  31.1 4.4 %collective-permute-done.4 = bf16[96,256]{1,0:T(8,128)(2,1)S(1)} collective-permute-done((bf16[96,256]{1,0:T(8,128)(2,1)S(1)}, bf16[96,256]{1,0:T(8,128)(2,1)S(1)}, u32[]{:S(2)}, u32[]{:S(2)}) %collective-permute-start.4) | collective-permute-done | bytes 49184 | tf_op jit(solution)/shard_map/ppermute | solution.py:272
  35.6 1.0 %collective-permute-start.9 = (bf16[96,256]{1,0:T(8,128)(2,1)S(1)}, bf16[96,256]{1,0:T(8,128)(2,1)S(1)}, u32[]{:S(2)}, u32[]{:S(2)}) collective-permute-start(bf16[96,256]{1,0:T(8,128)(2,1)S(1)} %add_convert_fusion.refs_0_), channel_id=1, source_target_pairs={{0,48},{16,32},{32,16},{48,0},{1,49},{17,33},{33,17},{49,1},{2,50}... | collective-permute-start | bytes 147464 | tf_op jit(solution)/shard_map/ppermute | solution.py:272
  36.6 2.9 %collective-permute-start.7 = (bf16[96,256]{1,0:T(8,128)(2,1)S(1)}, bf16[96,256]{1,0:T(8,128)(2,1)S(1)}, u32[]{:S(2)}, u32[]{:S(2)}) collective-permute-start(bf16[96,256]{1,0:T(8,128)(2,1)S(1)} %add_convert_fusion.refs_0_), channel_id=1, source_target_pairs={{0,32},{16,48},{32,0},{48,16},{1,33},{17,49},{33,1},{49,17},{2,34}... | collective-permute-start | bytes 147464 | tf_op jit(solution)/shard_map/ppermute | solution.py:272
  39.5 0.3 collective-permute-done.9.refs_3_
  39.8 1.7 %collective-permute-done.7.refs_1_ = bf16[96,256]{1,0:T(8,128)(2,1)S(1)} collective-permute-done((bf16[96,256]{1,0:T(8,128)(2,1)S(1)}, bf16[96,256]{1,0:T(8,128)(2,1)S(1)}, u32[]{:S(2)}, u32[]{:S(2)}) %collective-permute-start.7) | collective-permute-done | bytes 49184 | tf_op jit(solution)/shard_map/ppermute | solution.py:272
  41.5 4.7 %collective-permute-start.10 = (bf16[96,1024]{1,0:T(8,128)(2,1)S(1)}, bf16[96,1024]{1,0:T(8,128)(2,1)S(1)}, u32[]{:S(2)}, u32[]{:S(2)}) collective-permute-start(bf16[96,1024]{1,0:T(8,128)(2,1)S(1)} %pad_maximum_fusion), channel_id=1, source_target_pairs={{0,8},{8,0},{1,9},{9,1},{2,10},{10,2},{3,11},{11,3},{4,12},{12,4},... | collective-permute-start | bytes 589832 | tf_op jit(solution)/shard_map/ppermute | solution.py:272
  46.2 1.1 %collective-permute-done.10.refs_4_ = bf16[96,1024]{1,0:T(8,128)(2,1)S(1)} collective-permute-done((bf16[96,1024]{1,0:T(8,128)(2,1)S(1)}, bf16[96,1024]{1,0:T(8,128)(2,1)S(1)}, u32[]{:S(2)}, u32[]{:S(2)}) %collective-permute-start.10) | collective-permute-done | bytes 196640 | tf_op jit(solution)/shard_map/ppermute | solution.py:272
  47.3 0.5 product.1
  47.8 9.8 %all_to_all.5.shares_ref = bf16[8,48,128]{2,1,0:T(8,128)(2,1)S(1)} all-to-all(bf16[8,48,128]{2,1,0:T(8,128)(2,1)S(1)} %product.1), channel_id=1, replica_groups=mesh['zh'=4,'x'=4,'core'=2,'y'=4,'zl'=2] {'y','zl'}, dimensions={0} | all-to-all | bytes 196608 | tf_op jit(solution)/shard_map/all_to_all | solution.py:300
  57.6 0.8 %finish.1 = f32[64,96]{1,0:T(8,128)} custom-call(bf16[8,48,128]{2,1,0:T(8,128)(2,1)S(1)} %all_to_all.5.shares_ref), custom_call_target="tpu_custom_call" | custom-call | tf_op jit(solution)/shard_map/finish/pallas_call | solution.py:260
  (16 shorter events, 0.1 us)
Async XLA Ops:
  0.0 6.5 %collective-permute-start.1 = (bf16[96,4096]{1,0:T(8,128)(2,1)}, bf16[96,4096]{1,0:T(8,128)(2,1)S(1)}, u32[]{:S(2)}, u32[]{:S(2)}) collective-permute-start(bf16[96,4096]{1,0:T(8,128)(2,1)} %sens_in.1), channel_id=1, source_target_pairs={{0,8},{8,0},{1,9},{9,1},{2,10},{10,2},{3,11},{11,3},{4,12},{12,4},... | collective-permute-start | bytes 2359304 | tf_op jit(solution)/shard_map/ppermute | solution.py:272
  3.2 3.3 %collective-permute-start = (f32[3,4096]{1,0:T(4,128)}, f32[3,4096]{1,0:T(4,128)S(1)}, u32[]{:S(2)}, u32[]{:S(2)}) collective-permute-start(f32[3,4096]{1,0:T(4,128)} %node_in.1), channel_id=1, source_target_pairs={{0,8},{8,0},{1,9},{9,1},{2,10},{10,2},{3,11},{11,3},{4,12},{12,4},... | collective-permute-start | bytes 147464 | tf_op jit(solution)/shard_map/ppermute | solution.py:272
  12.5 4.1 %collective-permute-start.2 = (bf16[96,512]{1,0:T(8,128)(2,1)S(1)}, bf16[96,512]{1,0:T(8,128)(2,1)S(1)}, u32[]{:S(2)}, u32[]{:S(2)}) collective-permute-start(bf16[96,512]{1,0:T(8,128)(2,1)S(1)} %pad_maximum_fusion.1), channel_id=1, source_target_pairs={{0,16},{16,0},{32,48},{48,32},{1,17},{17,1},{33,49},{49,33},{2,18}... | collective-permute-start | bytes 294920 | tf_op jit(solution)/shard_map/ppermute | solution.py:272
  16.6 30.7 %copy-start = (bf16[2048,512]{1,0:T(8,128)(2,1)S(1)}, bf16[2048,512]{1,0:T(8,128)(2,1)}, u32[]{:S(2)}) copy-start(bf16[2048,512]{1,0:T(8,128)(2,1)} %refs_5_.1) | copy-start | bytes 6291460
  16.6 4.3 %collective-permute-start.3 = (bf16[96,256]{1,0:T(8,128)(2,1)S(1)}, bf16[96,256]{1,0:T(8,128)(2,1)S(1)}, u32[]{:S(2)}, u32[]{:S(2)}) collective-permute-start(bf16[96,256]{1,0:T(8,128)(2,1)S(1)} %fusion), channel_id=1, source_target_pairs={{0,48},{16,32},{32,16},{48,0},{1,49},{17,33},{33,17},{49,1},{2,50}... | collective-permute-start | bytes 147464 | tf_op jit(solution)/shard_map/ppermute | solution.py:272
  21.0 8.3 %collective-permute-start.6 = (bf16[96,256]{1,0:T(8,128)(2,1)S(1)}, bf16[96,256]{1,0:T(8,128)(2,1)S(1)}, u32[]{:S(2)}, u32[]{:S(2)}) collective-permute-start(bf16[96,256]{1,0:T(8,128)(2,1)S(1)} %fusion.2), channel_id=1, source_target_pairs={{0,192},{64,128},{128,64},{192,0},{1,193},{65,129},{129,65},{193,1... | collective-permute-start | bytes 147464 | tf_op jit(solution)/shard_map/ppermute | solution.py:272
  27.1 4.0 %collective-permute-start.5 = (bf16[96,256]{1,0:T(8,128)(2,1)S(1)}, bf16[96,256]{1,0:T(8,128)(2,1)S(1)}, u32[]{:S(2)}, u32[]{:S(2)}) collective-permute-start(bf16[96,256]{1,0:T(8,128)(2,1)S(1)} %fusion.2), channel_id=1, source_target_pairs={{0,64},{64,0},{128,192},{192,128},{1,65},{65,1},{129,193},{193,129... | collective-permute-start | bytes 147464 | tf_op jit(solution)/shard_map/ppermute | solution.py:272
  28.3 7.3 %collective-permute-start.4 = (bf16[96,256]{1,0:T(8,128)(2,1)S(1)}, bf16[96,256]{1,0:T(8,128)(2,1)S(1)}, u32[]{:S(2)}, u32[]{:S(2)}) collective-permute-start(bf16[96,256]{1,0:T(8,128)(2,1)S(1)} %fusion.2), channel_id=1, source_target_pairs={{0,128},{64,192},{128,0},{192,64},{1,129},{65,193},{129,1},{193,65... | collective-permute-start | bytes 147464 | tf_op jit(solution)/shard_map/ppermute | solution.py:272
  35.6 4.2 %collective-permute-start.9 = (bf16[96,256]{1,0:T(8,128)(2,1)S(1)}, bf16[96,256]{1,0:T(8,128)(2,1)S(1)}, u32[]{:S(2)}, u32[]{:S(2)}) collective-permute-start(bf16[96,256]{1,0:T(8,128)(2,1)S(1)} %add_convert_fusion.refs_0_), channel_id=1, source_target_pairs={{0,48},{16,32},{32,16},{48,0},{1,49},{17,33},{33,17},{49,1},{2,50}... | collective-permute-start | bytes 147464 | tf_op jit(solution)/shard_map/ppermute | solution.py:272
  36.6 3.2 %collective-permute-start.8 = (bf16[96,256]{1,0:T(8,128)(2,1)S(1)}, bf16[96,256]{1,0:T(8,128)(2,1)S(1)}, u32[]{:S(2)}, u32[]{:S(2)}) collective-permute-start(bf16[96,256]{1,0:T(8,128)(2,1)S(1)} %add_convert_fusion.refs_0_), channel_id=1, source_target_pairs={{0,16},{16,0},{32,48},{48,32},{1,17},{17,1},{33,49},{49,33},{2,18}... | collective-permute-start | bytes 147464 | tf_op jit(solution)/shard_map/ppermute | solution.py:272
  36.6 4.9 %collective-permute-start.7 = (bf16[96,256]{1,0:T(8,128)(2,1)S(1)}, bf16[96,256]{1,0:T(8,128)(2,1)S(1)}, u32[]{:S(2)}, u32[]{:S(2)}) collective-permute-start(bf16[96,256]{1,0:T(8,128)(2,1)S(1)} %add_convert_fusion.refs_0_), channel_id=1, source_target_pairs={{0,32},{16,48},{32,0},{48,16},{1,33},{17,49},{33,1},{49,17},{2,34}... | collective-permute-start | bytes 147464 | tf_op jit(solution)/shard_map/ppermute | solution.py:272
  41.5 5.8 %collective-permute-start.10 = (bf16[96,1024]{1,0:T(8,128)(2,1)S(1)}, bf16[96,1024]{1,0:T(8,128)(2,1)S(1)}, u32[]{:S(2)}, u32[]{:S(2)}) collective-permute-start(bf16[96,1024]{1,0:T(8,128)(2,1)S(1)} %pad_maximum_fusion), channel_id=1, source_target_pairs={{0,8},{8,0},{1,9},{9,1},{2,10},{10,2},{3,11},{11,3},{4,12},{12,4},... | collective-permute-start | bytes 589832 | tf_op jit(solution)/shard_map/ppermute | solution.py:272

commit v5 on v4

--- a/solution.py
+++ b/solution.py
@@ -211,13 +211,10 @@
     core = lax.axis_index("core")
     x = lax.axis_index("x")
     total = None
-    for half, joined in ((core, blocks[:-1]), (1 - core, blocks[-1:])):
-        for i, by in enumerate(order):
+    for i, half in enumerate((core, 1 - core)):
+        for joined, by in zip(blocks, order):
             at = pl.multiple_of((half * 4 + lax.bitwise_xor(x, by)) * span, span)
-            if len(joined) == 1:
-                block = joined[0][:, i * span : (i + 1) * span]
-            else:
-                block = joined[i][...]
+            block = joined[:, i * span : (i + 1) * span]
             term = jnp.dot(
                 block,
                 inverse_ref[pl.ds(at, span), :],
@@ -294,9 +291,9 @@
     mine = summed.astype(jnp.bfloat16)
 
     order = (2, 1, 3)
-    along_x = [mine] + [swapped(mine, "x", by) for by in order]
-    across = swapped(jnp.concatenate(along_x, axis=1), "core", 1)
-    shares = product((0,) + order, along_x + [across], inverse, 8)
+    both = jnp.concatenate([mine, swapped(mine, "core", 1)], axis=1)
+    along_x = [both] + [swapped(both, "x", by) for by in order]
+    shares = product((0,) + order, along_x, inverse, 8)
     arrived_shares = lax.all_to_all(
         shares, ("y", "zl"), split_axis=0, concat_axis=0, tiled=True
     )

time: 59.3 us -> 59.7 us (level)
  waiting for transfers between devices: 9.75 us -> 11.6 us
  starting transfers between devices: 21.3 us -> 19.6 us
    ppermute x11, waiting for transfers between devices: 9.75 us -> 11.6 us  [swapped(): return lax.ppermute(value, axis, [(i, i ^ by) for i in range(size)])]
    ppermute x11, starting transfers between devices: 21.3 us -> 19.6 us  [swapped(): return lax.ppermute(value, axis, [(i, i ^ by) for i in range(size)])]
  transfers between devices with their start and end apart: 11 -> 11, of which waited for: 6 -> 7; matrix products, arithmetic and copies ran while one was open for 0% -> 0% of each run, Pallas kernels for 17% -> 17%
where the time goes in v5:
time: 59.7 us; the launch traced here: 58.5 us
  starting transfers between devices  19.6 us (33%)
  Pallas kernels  17.3 us (29%)
  waiting for transfers between devices  11.6 us (19%)
  blocking collectives  9.76 us (16%)
    ppermute x11, starting transfers between devices, swapped(): return lax.ppermute(value, axis, [(i, i ^ by) for i in range(size)])  19.6 us
    ppermute x11, waiting for transfers between devices, swapped(): return lax.ppermute(value, axis, [(i, i ^ by) for i in range(size)])  11.6 us
    pallas_call x3, Pallas kernels, pull(): pl.pallas_call(functools.partial(pull_kernel, step), out_shape=jax.ShapeD...  10.1 us
    all_to_all x1, blocking collectives, per_device(): lax.all_to_all(shares, ('y', 'zl'), split_axis=0, concat_axis=0, tiled=True)  9.76 us
    pallas_call x1, Pallas kernels, first_pull(): pl.pallas_call(functools.partial(first_kernel, step), out_shape=[jax.Shap...  3.32 us
    pallas_call x1, Pallas kernels, second_pull(): pl.pallas_call(functools.partial(second_kernel, step), out_shape=[jax.Sha...  2.47 us
  transfers between devices with their start and end apart: 11, of which 7 were waited for; matrix products, arithmetic and copies ran while one was open for 0% of the time, Pallas kernels for 17%

profile of v5, /device:TPU:1, one launch (start us, length us, event | category | flops | bytes accessed | tf_op | source)
XLA Modules:
  0.0 58.5 jit_solution(9469420318384820333)
XLA Ops:
  0.0 3.2 %collective-permute-start.1 = (bf16[96,4096]{1,0:T(8,128)(2,1)}, bf16[96,4096]{1,0:T(8,128)(2,1)S(1)}, u32[]{:S(2)}, u32[]{:S(2)}) collective-permute-start(bf16[96,4096]{1,0:T(8,128)(2,1)} %sens_in.1), channel_id=1, source_target_pairs={{0,8},{8,0},{1,9},{9,1},{2,10},{10,2},{3,11},{11,3},{4,12},{12,4},... | collective-permute-start | bytes 2359304 | tf_op jit(solution)/shard_map/ppermute | solution.py:269
  3.2 3.3 %first_pull.1 = (f32[96,256]{1,0:T(8,128)S(1)}, bf16[4096,128]{1,0:T(8,128)(2,1)S(1)}, bf16[96,4096]{1,0:T(8,128)(2,1)S(1)}, bf16[128,2048]{1,0:T(8,128)(2,1)S(1)}) custom-call(bf16[96,4096]{1,0:T(8,128)(2,1)} %sens_in.1, f32[3,4096]{1,0:T(4,128)} %node_in.1, f32[3,2048]{1,0:T(4,128)} %ctrl_in.1), custom_call_target="tpu_custom_call" | custom-call | flops 419430400 | bytes 1835008 | tf_op jit(solution)/shard_map/first_pull/pallas_call | solution.py:138
  6.5 2.5 %second_pull.1 = (f32[96,256]{1,0:T(8,128)S(1)}, bf16[4096,128]{1,0:T(8,128)(2,1)S(1)}) custom-call(f32[96,256]{1,0:T(8,128)S(1)} %get-tuple-element.13.part_ref, f32[3,4096]{1,0:T(4,128)S(1)} %collective-permute-done.node_xyz, bf16[96,4096]{1,0:T(8,128)(2,1)S(1)} %collective-permute-done.1.sens_ref.sens_b, bf16[128,2048]{1,0:T(8,128)(2,1)S(1)} %get-tuple-element.14.ctrl_ref), custom_call_target="tpu_custom_call" | custom-call | flops 419430400 | bytes 1835008 | tf_op jit(solution)/shard_map/second_pull/pallas_call | solution.py:174
  9.0 3.4 %pull.4 = f32[96,256]{1,0:T(8,128)S(1)} custom-call(bf16[4096,128]{1,0:T(8,128)(2,1)S(1)} %get-tuple-element.11.node_a, bf16[96,4096]{1,0:T(8,128)(2,1)S(1)} %get-tuple-element.12.sens_a, bf16[4096,128]{1,0:T(8,128)(2,1)S(1)} %get-tuple-element.15.node_b, bf16[96,4096]{1,0:T(8,128)(2,1)S(1)} %collective-permute-done.1.sens_ref.sens_b, ...), custom_call_target="tpu_custom_call" | custom-call | flops 838860800 | bytes 1835008 | tf_op jit(solution)/shard_map/pull/pallas_call | solution.py:197
  12.5 0.3 collective-permute-start.2
  12.7 3.4 %pull.5 = f32[96,256]{1,0:T(8,128)S(1)} custom-call(bf16[4096,128]{1,0:T(8,128)(2,1)S(1)} %get-tuple-element.11.node_a, bf16[96,4096]{1,0:T(8,128)(2,1)S(1)} %get-tuple-element.12.sens_a, bf16[4096,128]{1,0:T(8,128)(2,1)S(1)} %get-tuple-element.15.node_b, bf16[96,4096]{1,0:T(8,128)(2,1)S(1)} %collective-permute-done.1.sens_ref.sens_b, ...), custom_call_target="tpu_custom_call" | custom-call | flops 838860800 | bytes 1835008 | tf_op jit(solution)/shard_map/pull/pallas_call | solution.py:197
  16.1 0.4 collective-permute-done.2
  16.6 0.9 %collective-permute-start.3 = (bf16[96,256]{1,0:T(8,128)(2,1)S(1)}, bf16[96,256]{1,0:T(8,128)(2,1)S(1)}, u32[]{:S(2)}, u32[]{:S(2)}) collective-permute-start(bf16[96,256]{1,0:T(8,128)(2,1)S(1)} %fusion), channel_id=1, source_target_pairs={{0,48},{16,32},{32,16},{48,0},{1,49},{17,33},{33,17},{49,1},{2,50}... | collective-permute-start | bytes 147464 | tf_op jit(solution)/shard_map/ppermute | solution.py:269
  17.6 3.4 %pull.3 = f32[96,256]{1,0:T(8,128)S(1)} custom-call(bf16[4096,128]{1,0:T(8,128)(2,1)S(1)} %get-tuple-element.11.node_a, bf16[96,4096]{1,0:T(8,128)(2,1)S(1)} %get-tuple-element.12.sens_a, bf16[4096,128]{1,0:T(8,128)(2,1)S(1)} %get-tuple-element.15.node_b, bf16[96,4096]{1,0:T(8,128)(2,1)S(1)} %collective-permute-done.1.sens_ref.sens_b, ...), custom_call_target="tpu_custom_call" | custom-call | flops 838860800 | bytes 1835008 | tf_op jit(solution)/shard_map/pull/pallas_call | solution.py:197
  21.0 6.1 %collective-permute-start.6 = (bf16[96,256]{1,0:T(8,128)(2,1)S(1)}, bf16[96,256]{1,0:T(8,128)(2,1)S(1)}, u32[]{:S(2)}, u32[]{:S(2)}) collective-permute-start(bf16[96,256]{1,0:T(8,128)(2,1)S(1)} %fusion.2), channel_id=1, source_target_pairs={{0,192},{64,128},{128,64},{192,0},{1,193},{65,129},{129,65},{193,1... | collective-permute-start | bytes 147464 | tf_op jit(solution)/shard_map/ppermute | solution.py:269
  27.1 1.2 %collective-permute-start.5 = (bf16[96,256]{1,0:T(8,128)(2,1)S(1)}, bf16[96,256]{1,0:T(8,128)(2,1)S(1)}, u32[]{:S(2)}, u32[]{:S(2)}) collective-permute-start(bf16[96,256]{1,0:T(8,128)(2,1)S(1)} %fusion.2), channel_id=1, source_target_pairs={{0,64},{64,0},{128,192},{192,128},{1,65},{65,1},{129,193},{193,129... | collective-permute-start | bytes 147464 | tf_op jit(solution)/shard_map/ppermute | solution.py:269
  28.3 1.0 %collective-permute-start.4 = (bf16[96,256]{1,0:T(8,128)(2,1)S(1)}, bf16[96,256]{1,0:T(8,128)(2,1)S(1)}, u32[]{:S(2)}, u32[]{:S(2)}) collective-permute-start(bf16[96,256]{1,0:T(8,128)(2,1)S(1)} %fusion.2), channel_id=1, source_target_pairs={{0,128},{64,192},{128,0},{192,64},{1,129},{65,193},{129,1},{193,65... | collective-permute-start | bytes 147464 | tf_op jit(solution)/shard_map/ppermute | solution.py:269
  29.3 1.8 %collective-permute-done.5 = bf16[96,256]{1,0:T(8,128)(2,1)S(1)} collective-permute-done((bf16[96,256]{1,0:T(8,128)(2,1)S(1)}, bf16[96,256]{1,0:T(8,128)(2,1)S(1)}, u32[]{:S(2)}, u32[]{:S(2)}) %collective-permute-start.5) | collective-permute-done | bytes 49184 | tf_op jit(solution)/shard_map/ppermute | solution.py:269
  31.1 4.4 %collective-permute-done.4 = bf16[96,256]{1,0:T(8,128)(2,1)S(1)} collective-permute-done((bf16[96,256]{1,0:T(8,128)(2,1)S(1)}, bf16[96,256]{1,0:T(8,128)(2,1)S(1)}, u32[]{:S(2)}, u32[]{:S(2)}) %collective-permute-start.4) | collective-permute-done | bytes 49184 | tf_op jit(solution)/shard_map/ppermute | solution.py:269
  35.6 3.0 %collective-permute-start.7 = (bf16[96,256]{1,0:T(8,128)(2,1)S(1)}, bf16[96,256]{1,0:T(8,128)(2,1)S(1)}, u32[]{:S(2)}, u32[]{:S(2)}) collective-permute-start(bf16[96,256]{1,0:T(8,128)(2,1)S(1)} %add_convert_fusion), channel_id=1, source_target_pairs={{0,8},{8,0},{1,9},{9,1},{2,10},{10,2},{3,11},{11,3},{4,12},{12,4},... | collective-permute-start | bytes 147464 | tf_op jit(solution)/shard_map/ppermute | solution.py:269
  38.6 0.9 %collective-permute-done.7 = bf16[96,256]{1,0:T(8,128)(2,1)S(1)} collective-permute-done((bf16[96,256]{1,0:T(8,128)(2,1)S(1)}, bf16[96,256]{1,0:T(8,128)(2,1)S(1)}, u32[]{:S(2)}, u32[]{:S(2)}) %collective-permute-start.7) | collective-permute-done | bytes 49184 | tf_op jit(solution)/shard_map/ppermute | solution.py:269
  39.5 1.7 %collective-permute-start.10 = (bf16[96,512]{1,0:T(8,128)(2,1)S(1)}, bf16[96,512]{1,0:T(8,128)(2,1)S(1)}, u32[]{:S(2)}, u32[]{:S(2)}) collective-permute-start(bf16[96,512]{1,0:T(8,128)(2,1)S(1)} %pad_maximum_fusion.1.refs_0_), channel_id=1, source_target_pairs={{0,48},{16,32},{32,16},{48,0},{1,49},{17,33},{33,17},{49,1},{2,50}... | collective-permute-start | bytes 294920 | tf_op jit(solution)/shard_map/ppermute | solution.py:269
  41.2 2.2 %collective-permute-start.8 = (bf16[96,512]{1,0:T(8,128)(2,1)S(1)}, bf16[96,512]{1,0:T(8,128)(2,1)S(1)}, u32[]{:S(2)}, u32[]{:S(2)}) collective-permute-start(bf16[96,512]{1,0:T(8,128)(2,1)S(1)} %pad_maximum_fusion.1.refs_0_), channel_id=1, source_target_pairs={{0,32},{16,48},{32,0},{48,16},{1,33},{17,49},{33,1},{49,17},{2,34}... | collective-permute-start | bytes 294920 | tf_op jit(solution)/shard_map/ppermute | solution.py:269
  43.4 1.3 %collective-permute-done.10.refs_3_ = bf16[96,512]{1,0:T(8,128)(2,1)S(1)} collective-permute-done((bf16[96,512]{1,0:T(8,128)(2,1)S(1)}, bf16[96,512]{1,0:T(8,128)(2,1)S(1)}, u32[]{:S(2)}, u32[]{:S(2)}) %collective-permute-start.10) | collective-permute-done | bytes 98336 | tf_op jit(solution)/shard_map/ppermute | solution.py:269
  44.7 0.2 collective-permute-done.9.refs_2_
  44.9 2.5 %collective-permute-done.8.refs_1_ = bf16[96,512]{1,0:T(8,128)(2,1)S(1)} collective-permute-done((bf16[96,512]{1,0:T(8,128)(2,1)S(1)}, bf16[96,512]{1,0:T(8,128)(2,1)S(1)}, u32[]{:S(2)}, u32[]{:S(2)}) %collective-permute-start.8) | collective-permute-done | bytes 98336 | tf_op jit(solution)/shard_map/ppermute | solution.py:269
  47.4 0.5 product.1
  48.0 9.8 %all_to_all.5.shares_ref = bf16[8,48,128]{2,1,0:T(8,128)(2,1)S(1)} all-to-all(bf16[8,48,128]{2,1,0:T(8,128)(2,1)S(1)} %product.1), channel_id=1, replica_groups=mesh['zh'=4,'x'=4,'core'=2,'y'=4,'zl'=2] {'y','zl'}, dimensions={0} | all-to-all | bytes 196608 | tf_op jit(solution)/shard_map/all_to_all | solution.py:297
  57.7 0.8 %finish.1 = f32[64,96]{1,0:T(8,128)} custom-call(bf16[8,48,128]{2,1,0:T(8,128)(2,1)S(1)} %all_to_all.5.shares_ref), custom_call_target="tpu_custom_call" | custom-call | tf_op jit(solution)/shard_map/finish/pallas_call | solution.py:257
  (16 shorter events, 0.1 us)
Async XLA Ops:
  0.0 6.5 %collective-permute-start.1 = (bf16[96,4096]{1,0:T(8,128)(2,1)}, bf16[96,4096]{1,0:T(8,128)(2,1)S(1)}, u32[]{:S(2)}, u32[]{:S(2)}) collective-permute-start(bf16[96,4096]{1,0:T(8,128)(2,1)} %sens_in.1), channel_id=1, source_target_pairs={{0,8},{8,0},{1,9},{9,1},{2,10},{10,2},{3,11},{11,3},{4,12},{12,4},... | collective-permute-start | bytes 2359304 | tf_op jit(solution)/shard_map/ppermute | solution.py:269
  3.2 3.3 %collective-permute-start = (f32[3,4096]{1,0:T(4,128)}, f32[3,4096]{1,0:T(4,128)S(1)}, u32[]{:S(2)}, u32[]{:S(2)}) collective-permute-start(f32[3,4096]{1,0:T(4,128)} %node_in.1), channel_id=1, source_target_pairs={{0,8},{8,0},{1,9},{9,1},{2,10},{10,2},{3,11},{11,3},{4,12},{12,4},... | collective-permute-start | bytes 147464 | tf_op jit(solution)/shard_map/ppermute | solution.py:269
  12.5 4.1 %collective-permute-start.2 = (bf16[96,512]{1,0:T(8,128)(2,1)S(1)}, bf16[96,512]{1,0:T(8,128)(2,1)S(1)}, u32[]{:S(2)}, u32[]{:S(2)}) collective-permute-start(bf16[96,512]{1,0:T(8,128)(2,1)S(1)} %pad_maximum_fusion), channel_id=1, source_target_pairs={{0,16},{16,0},{32,48},{48,32},{1,17},{17,1},{33,49},{49,33},{2,18}... | collective-permute-start | bytes 294920 | tf_op jit(solution)/shard_map/ppermute | solution.py:269
  16.6 30.8 %copy-start = (bf16[2048,512]{1,0:T(8,128)(2,1)S(1)}, bf16[2048,512]{1,0:T(8,128)(2,1)}, u32[]{:S(2)}) copy-start(bf16[2048,512]{1,0:T(8,128)(2,1)} %refs_4_.1) | copy-start | bytes 6291460
  16.6 4.3 %collective-permute-start.3 = (bf16[96,256]{1,0:T(8,128)(2,1)S(1)}, bf16[96,256]{1,0:T(8,128)(2,1)S(1)}, u32[]{:S(2)}, u32[]{:S(2)}) collective-permute-start(bf16[96,256]{1,0:T(8,128)(2,1)S(1)} %fusion), channel_id=1, source_target_pairs={{0,48},{16,32},{32,16},{48,0},{1,49},{17,33},{33,17},{49,1},{2,50}... | collective-permute-start | bytes 147464 | tf_op jit(solution)/shard_map/ppermute | solution.py:269
  21.0 8.3 %collective-permute-start.6 = (bf16[96,256]{1,0:T(8,128)(2,1)S(1)}, bf16[96,256]{1,0:T(8,128)(2,1)S(1)}, u32[]{:S(2)}, u32[]{:S(2)}) collective-permute-start(bf16[96,256]{1,0:T(8,128)(2,1)S(1)} %fusion.2), channel_id=1, source_target_pairs={{0,192},{64,128},{128,64},{192,0},{1,193},{65,129},{129,65},{193,1... | collective-permute-start | bytes 147464 | tf_op jit(solution)/shard_map/ppermute | solution.py:269
  27.1 4.0 %collective-permute-start.5 = (bf16[96,256]{1,0:T(8,128)(2,1)S(1)}, bf16[96,256]{1,0:T(8,128)(2,1)S(1)}, u32[]{:S(2)}, u32[]{:S(2)}) collective-permute-start(bf16[96,256]{1,0:T(8,128)(2,1)S(1)} %fusion.2), channel_id=1, source_target_pairs={{0,64},{64,0},{128,192},{192,128},{1,65},{65,1},{129,193},{193,129... | collective-permute-start | bytes 147464 | tf_op jit(solution)/shard_map/ppermute | solution.py:269
  28.3 7.3 %collective-permute-start.4 = (bf16[96,256]{1,0:T(8,128)(2,1)S(1)}, bf16[96,256]{1,0:T(8,128)(2,1)S(1)}, u32[]{:S(2)}, u32[]{:S(2)}) collective-permute-start(bf16[96,256]{1,0:T(8,128)(2,1)S(1)} %fusion.2), channel_id=1, source_target_pairs={{0,128},{64,192},{128,0},{192,64},{1,129},{65,193},{129,1},{193,65... | collective-permute-start | bytes 147464 | tf_op jit(solution)/shard_map/ppermute | solution.py:269
  35.6 3.9 %collective-permute-start.7 = (bf16[96,256]{1,0:T(8,128)(2,1)S(1)}, bf16[96,256]{1,0:T(8,128)(2,1)S(1)}, u32[]{:S(2)}, u32[]{:S(2)}) collective-permute-start(bf16[96,256]{1,0:T(8,128)(2,1)S(1)} %add_convert_fusion), channel_id=1, source_target_pairs={{0,8},{8,0},{1,9},{9,1},{2,10},{10,2},{3,11},{11,3},{4,12},{12,4},... | collective-permute-start | bytes 147464 | tf_op jit(solution)/shard_map/ppermute | solution.py:269
  39.5 5.2 %collective-permute-start.10 = (bf16[96,512]{1,0:T(8,128)(2,1)S(1)}, bf16[96,512]{1,0:T(8,128)(2,1)S(1)}, u32[]{:S(2)}, u32[]{:S(2)}) collective-permute-start(bf16[96,512]{1,0:T(8,128)(2,1)S(1)} %pad_maximum_fusion.1.refs_0_), channel_id=1, source_target_pairs={{0,48},{16,32},{32,16},{48,0},{1,49},{17,33},{33,17},{49,1},{2,50}... | collective-permute-start | bytes 294920 | tf_op jit(solution)/shard_map/ppermute | solution.py:269
  41.2 3.8 %collective-permute-start.9 = (bf16[96,512]{1,0:T(8,128)(2,1)S(1)}, bf16[96,512]{1,0:T(8,128)(2,1)S(1)}, u32[]{:S(2)}, u32[]{:S(2)}) collective-permute-start(bf16[96,512]{1,0:T(8,128)(2,1)S(1)} %pad_maximum_fusion.1.refs_0_), channel_id=1, source_target_pairs={{0,16},{16,0},{32,48},{48,32},{1,17},{17,1},{33,49},{49,33},{2,18}... | collective-permute-start | bytes 294920 | tf_op jit(solution)/shard_map/ppermute | solution.py:269
  41.2 6.2 %collective-permute-start.8 = (bf16[96,512]{1,0:T(8,128)(2,1)S(1)}, bf16[96,512]{1,0:T(8,128)(2,1)S(1)}, u32[]{:S(2)}, u32[]{:S(2)}) collective-permute-start(bf16[96,512]{1,0:T(8,128)(2,1)S(1)} %pad_maximum_fusion.1.refs_0_), channel_id=1, source_target_pairs={{0,32},{16,48},{32,0},{48,16},{1,33},{17,49},{33,1},{49,17},{2,34}... | collective-permute-start | bytes 294920 | tf_op jit(solution)/shard_map/ppermute | solution.py:269
